TPU v7x, 32 devices: a whole 2x2x4 slice. The times are simulated.
32 devices in a mesh: row: 4 (over y, x), seq: 8 (over z, core).
Axes of the slice: x: 2, y: 2, z: 4, core: 2. Of those that a mesh axis runs over, the one named last changes fastest.
Arguments:
- hidden_in: bfloat16 [4, 1024, 2048], P('row', 'seq'), may hold values from -6 to 6
- positions: int32 [4, 1024], P('row', 'seq'), may hold values from 0 to 7164, as said below
- languages: int32 [4], replicated, may hold values from 0 to 6
- ln1_gain: bfloat16 [2048], replicated, may hold values from 0.5 to 1.5
- ln1_bias: bfloat16 [2048], replicated, may hold values from -1.1953125 to 1.1953125
- w_qkv: bfloat16 [2048, 6144], P(None, 'seq'), may hold values from -0.125 to 0.125
- b_qkv: bfloat16 [6144], P('seq'), may hold values from -1.1953125 to 1.1953125
- w_out: bfloat16 [2048, 2048], P('seq'), may hold values from -3 to 3
- ln2_gain: bfloat16 [2048], replicated, may hold values from 0.5 to 1.5
- ln2_bias: bfloat16 [2048], replicated, may hold values from -1.1953125 to 1.1953125
- w_gate: bfloat16 [2048, 5632], P(None, 'seq'), may hold values from -0.125 to 0.125
- w_up: bfloat16 [2048, 5632], P(None, 'seq'), may hold values from -0.125 to 0.125
- w_down: bfloat16 [5632, 2048], P('seq'), may hold values from -0.078125 to 0.078125
- cotangent: bfloat16 [4, 1024, 2048], P('row', 'seq'), may hold values from -6 to 6
Outputs:
- output: bfloat16 [4, 1024, 2048], P('row', 'seq')
- input_grad: bfloat16 [4, 1024, 2048], P('row', 'seq')
- grad_ln1_gain: float32 [2048], P('seq')
- grad_ln1_bias: float32 [2048], P('seq')
- grad_w_qkv: float32 [2048, 6144], P(None, 'seq')
- grad_b_qkv: float32 [6144], P('seq')
- grad_w_out: float32 [2048, 2048], P('seq')
- grad_ln2_gain: float32 [2048], P('seq')
- grad_ln2_bias: float32 [2048], P('seq')
- grad_w_gate: float32 [2048, 5632], P(None, 'seq')
- grad_w_up: float32 [2048, 5632], P(None, 'seq')
- grad_w_down: float32 [5632, 2048], P('seq')
Inputs may be any that keep to these rules, and one draw needn't show every extreme that they name: Each sequence's positions start at an offset of 0 to 4095 and rise by 1 to 3 from one token to the next; some sequence starts at 0, and another starts at 4095 and rises by 3 at every token.
All inputs are finite; a program needn't handle non-finite values.
Results may differ from a plain program's by a relative error of at most 0.013.
Values may be sent and summed in bfloat16 or wider, within the bound.
No kernel may reach another device: no remote copies, remote signals or barrier semaphores. Data moves between devices by JAX's collectives and lax.ppermute only.
A program may use at most 256 MiB of HBM per device.

v0:
```python
import jax
import jax.numpy as jnp
from jax import lax
from jax.experimental import pallas as pl
from jax.experimental.pallas import tpu as pltpu
from jax.sharding import PartitionSpec as P


HEAD_DIM = 64
ROT = 16
LANGS = 7
CORES = 2
LANES = 128
QBLOCK = 256
SPLITS = 2
BIAS_ROWS = 16

EPS = 1e-05
NEG = -1e30
BASE = 10000.0

F32 = jnp.float32
BF16 = jnp.bfloat16


def standardize(values):
    center = values - jnp.mean(values, -1, keepdims=True)
    spread = jnp.mean(center * center, -1, keepdims=True)
    inverse = lax.rsqrt(spread + EPS)
    return (center * inverse, inverse)


def norm_back(grad_normed, normed, inverse):
    return inverse * (
        grad_normed
        - jnp.mean(grad_normed, -1, keepdims=True)
        - normed * jnp.mean(grad_normed * normed, -1, keepdims=True)
    )


def mm(left, right, dims=((1,), (0,))):
    return lax.dot_general(left, right, (dims, ((), ())), preferred_element_type=F32)


def pick(array, at, axis=0):
    return lax.dynamic_index_in_dim(array, at, axis, keepdims=False)


def rows_of(array, start, size):
    return lax.dynamic_slice_in_dim(array, start, size, 0)


def swap_cores(value):
    size = lax.axis_size("seq")
    return lax.ppermute(value, "seq", [(d, d ^ 1) for d in range(size)])


def ring(value):
    size = lax.axis_size("seq")
    to = [(d, (d + CORES) % size) for d in range(size)]
    return [lax.ppermute(part, "seq", to) for part in value]


def cut(value):
    rows = value.shape[0] // SPLITS
    return [value[k * rows : (k + 1) * rows] for k in range(SPLITS)]


def after(value, *earlier):
    return lax.optimization_barrier((value,) + earlier)[0]


def gather_places(local):
    size = lax.axis_size("seq")
    me = lax.axis_index("seq")
    have, bit = local, 1
    while bit < size:
        other = lax.ppermute(have, "seq", [(d, d ^ bit) for d in range(size)])
        own = (me // bit) % 2
        have = jnp.where(
            own == 0, jnp.concatenate([have, other]), jnp.concatenate([other, have])
        )
        bit *= 2
    return have


def gather_tokens(local):
    size = lax.axis_size("seq")
    me = lax.axis_index("seq")
    chips = size // CORES
    chip, core = me // CORES, me % CORES
    count = local.shape[0]
    full = jnp.zeros((size * count,) + local.shape[1:], local.dtype)
    piece = cut(local)
    for step in range(chips):
        following = ring(piece) if step + 1 < chips else None
        base = ((chip - step) % chips) * CORES
        rows = count // SPLITS
        for k, part in enumerate(piece):
            other = swap_cores(part)
            full = lax.dynamic_update_slice_in_dim(full, part, (base + core) * count + k * rows, 0)
            full = lax.dynamic_update_slice_in_dim(
                full, other, (base + 1 - core) * count + k * rows, 0
            )
        piece = following
    return full


def scatter_tokens(block_of, count, meanwhile=None):
    size = lax.axis_size("seq")
    me = lax.axis_index("seq")
    chips = size // CORES
    chip, core = me // CORES, me % CORES
    rows = count // SPLITS
    carried = [None] * SPLITS
    for step in range(1, chips + 1):
        row = ((chip - step) % chips) * CORES * count
        if meanwhile is not None and step == 2:
            row = after(row, *meanwhile)
        block = block_of(row)
        totals = []
        for k in range(SPLITS):
            other = swap_cores(rows_of(block, (1 - core) * count + k * rows, rows).astype(BF16))
            total = rows_of(block, core * count + k * rows, rows) + other.astype(F32)
            if carried[k] is not None:
                total = total + carried[k].astype(F32)
            totals.append(total)
        if step < chips:
            carried = ring([total.astype(BF16) for total in totals])
    return jnp.concatenate(totals, 0)


def row_bits():
    size = lax.axis_size("row")
    return [1 << b for b in range(size.bit_length() - 1)]


def row_swap(value, bit):
    size = lax.axis_size("row")
    return lax.ppermute(value, "row", [(d, d ^ bit) for d in range(size)])


def side(bit):
    return (lax.axis_index("row") // bit) % 2


def flows_of():
    bits = row_bits()
    return [bits, bits[1:] + bits[:1]] if len(bits) > 1 else [bits]


def place_in(order):
    place = 0
    for bit in order:
        place = place * 2 + side(bit)
    return place


def row_scatter(value):
    flows = flows_of()
    done = []
    for number, order in enumerate(flows):
        rows = value.shape[0] // len(flows)
        part = value[number * rows : (number + 1) * rows]
        for bit in order:
            half = part.shape[0] // 2
            sent = row_swap(rows_of(part, (1 - side(bit)) * half, half), bit)
            kept = rows_of(part, side(bit) * half, half)
            part = (kept.astype(F32) + sent.astype(F32)).astype(value.dtype)
        done.append(part)
    return done


def row_gather(chunks, dtype):
    flows = flows_of()
    rows, columns = chunks[0].shape
    total = rows * lax.axis_size("row")
    full = jnp.zeros((total * len(flows), columns), dtype)
    for number, order in enumerate(flows):
        pieces = [(place_in(order), chunks[number])]
        for level, bit in enumerate(reversed(order)):
            flip = (1 - 2 * side(bit)) << level
            pieces = pieces + [(at + flip, row_swap(piece, bit)) for at, piece in pieces]
        for at, piece in pieces:
            full = lax.dynamic_update_slice_in_dim(
                full, piece.astype(dtype), number * total + at * rows, 0
            )
    return full


def own_chunks(value):
    flows = flows_of()
    total = value.shape[0] // len(flows)
    rows = total // lax.axis_size("row")
    return [
        rows_of(value, number * total + place_in(order) * rows, rows)
        for number, order in enumerate(flows)
    ]


def to_heads(units):
    size = lax.axis_size("seq")
    me = lax.axis_index("seq")
    unit = units.shape[-1] // 3
    got = jnp.stack(
        [
            lax.ppermute(
                units[..., i * unit : (i + 1) * unit],
                "seq",
                [(d, (3 * d + i) % size) for d in range(size)],
            )
            for i in range(3)
        ]
    )
    return [pick(got, (me + part * size) % 3) for part in range(3)]


def from_heads(parts):
    size = lax.axis_size("seq")
    me = lax.axis_index("seq")
    stacked = jnp.stack(parts)
    back = []
    for i in range(3):
        part = ((i - me) * pow(size, -1, 3)) % 3
        back.append(
            lax.ppermute(
                pick(stacked, part), "seq", [((3 * d + i) % size, d) for d in range(size)]
            )
        )
    return jnp.concatenate(back, -1)


def small_sums(values):
    size = lax.axis_size("seq")
    me = lax.axis_index("seq")
    part = values
    bit = size // 2
    while bit:
        own = (me // bit) % 2
        halves = part.reshape((2, part.shape[0] // 2) + part.shape[1:])
        part = pick(halves, own) + lax.ppermute(
            pick(halves, 1 - own), "seq", [(d, d ^ bit) for d in range(size)]
        )
        bit //= 2
    part = part[0]
    for bit in row_bits():
        part = part + row_swap(part, bit)
    return part


def turn(value, cosine, sine):
    lane = lax.broadcasted_iota(jnp.int32, sine.shape, 1) % HEAD_DIM
    half = ROT // 2
    low = jnp.where(lane < half, -sine, 0.0)
    high = jnp.where(lane < half, 0.0, sine)
    return (
        value * cosine
        + pltpu.roll(value, LANES - half, 1) * low
        + pltpu.roll(value, half, 1) * high
    )


def rotary_tables(places):
    half = ROT // 2
    freqs = BASE ** (-(jnp.arange(half, dtype=F32) * 2.0) / ROT)
    still = jnp.zeros(HEAD_DIM - ROT, F32)
    lanes = jnp.tile(jnp.concatenate([freqs, freqs, still]), LANES // HEAD_DIM)
    angles = places.astype(F32)[:, None] * lanes[None, :]
    return jnp.cos(angles), jnp.sin(angles)


def head_masks(rows):
    lane = lax.broadcasted_iota(jnp.int32, (rows, LANES), 1)
    return [lane // HEAD_DIM == h for h in range(LANES // HEAD_DIM)]


def causal(first, rows, keys):
    query = lax.broadcasted_iota(jnp.int32, (rows, keys), 0) + first
    key = lax.broadcasted_iota(jnp.int32, (rows, keys), 1)
    return key <= query


ROWS_COLS = ((1,), (1,))
COLS_COLS = ((0,), (0,))


def attend_kernel(
    q_in, k_in, v_in, bias, cosine, sine, out, q_out, k_out, v_out, stats
):
    length = q_in.shape[1]
    factor = float(HEAD_DIM) ** (-0.5)
    cos, sin = cosine[...], sine[...]
    q_out[0] = turn(q_in[0] + bias[0, 0:1], cos, sin).astype(BF16)
    k_out[0] = turn(k_in[0] + bias[0, 1:2], cos, sin).astype(BF16)
    v_out[0] = (v_in[0] + bias[0, 2:3]).astype(BF16)
    masks = head_masks(QBLOCK)
    for start in range(0, length, QBLOCK):
        end = start + QBLOCK
        query = q_out[0, start:end]
        key, value = k_out[0, 0:end], v_out[0, 0:end]
        keep = causal(start, QBLOCK, end)
        mixed, logs = None, None
        for mask in masks:
            logits = mm(jnp.where(mask, query, jnp.zeros_like(query)), key, ROWS_COLS) * factor
            logits = jnp.where(keep, logits, NEG)
            peak = jnp.max(logits, -1, keepdims=True)
            expo = jnp.exp(logits - peak)
            denom = jnp.sum(expo, -1, keepdims=True)
            part = mm((expo / denom).astype(BF16), value)
            log = jnp.broadcast_to(peak + jnp.log(denom), (QBLOCK, LANES))
            mixed = part if mixed is None else jnp.where(mask, part, mixed)
            logs = log if logs is None else jnp.where(mask, log, logs)
        out[0, start:end] = mixed.astype(BF16)
        stats[0, start:end] = logs


def attend_back_kernel(
    q_in, k_in, v_in, grad_in, stats, cosine, sine, dq_out, dk_out, dv_out, dk, dv
):
    length = q_in.shape[1]
    factor = float(HEAD_DIM) ** (-0.5)
    cos, sin = cosine[...], -sine[...]
    masks = head_masks(QBLOCK)
    dk[...] = jnp.zeros_like(dk)
    dv[...] = jnp.zeros_like(dv)
    for start in range(0, length, QBLOCK):
        end = start + QBLOCK
        query, grad = q_in[0, start:end], grad_in[0, start:end]
        key, value = k_in[0, 0:end], v_in[0, 0:end]
        keep = causal(start, QBLOCK, end)
        dq = None
        for number, mask in enumerate(masks):
            own_query = jnp.where(mask, query, jnp.zeros_like(query))
            own_grad = jnp.where(mask, grad, jnp.zeros_like(grad))
            log = stats[0, start:end, number * HEAD_DIM : number * HEAD_DIM + 1]
            logits = mm(own_query, key, ROWS_COLS) * factor
            probs = jnp.where(keep, jnp.exp(jnp.where(keep, logits, NEG) - log), 0.0)
            grad_probs = mm(own_grad, value, ROWS_COLS)
            inner = jnp.sum(grad_probs * probs, -1, keepdims=True)
            grad_logits = (probs * (grad_probs - inner)).astype(BF16)
            dv[0:end] += mm(probs.astype(BF16), own_grad, COLS_COLS)
            dk[0:end] += mm(grad_logits, own_query, COLS_COLS)
            part = mm(grad_logits, key)
            dq = part if dq is None else jnp.where(mask, part, dq)
        dq_out[0, start:end] = turn(dq * factor, cos[start:end], sin[start:end]).astype(BF16)
    dk_out[0] = turn(dk[...] * factor, cos, sin).astype(BF16)
    dv_out[0] = dv[...].astype(BF16)


def pair_spec(length):
    return pl.BlockSpec((1, length, LANES), lambda g: (0, 0, g))


def attend(parts, bias, tables):
    _, length, width = parts[0].shape
    spec = pair_spec(length)
    table = pl.BlockSpec((length, LANES), lambda g: (0, 0))
    shape = jax.ShapeDtypeStruct((1, length, width), BF16)
    return pl.pallas_call(
        attend_kernel,
        grid=(width // LANES,),
        in_specs=[spec] * 3
        + [pl.BlockSpec((1, 3, LANES), lambda g: (0, 0, g))]
        + [table] * 2,
        out_specs=[spec] * 5,
        out_shape=[shape] * 4 + [jax.ShapeDtypeStruct((1, length, width), F32)],
        name="attend",
    )(*parts, bias, *tables)


def attend_back(rotated, grad, stats, tables):
    _, length, width = grad.shape
    spec = pair_spec(length)
    table = pl.BlockSpec((length, LANES), lambda g: (0, 0))
    shape = jax.ShapeDtypeStruct((1, length, width), BF16)
    return pl.pallas_call(
        attend_back_kernel,
        grid=(width // LANES,),
        in_specs=[spec] * 5 + [table] * 2,
        out_specs=[spec] * 3,
        out_shape=[shape] * 3,
        scratch_shapes=[pltpu.VMEM((length, LANES), F32)] * 2,
        name="attend_back",
    )(*rotated, grad, stats, *tables)


def body(
    hidden_in,
    positions,
    languages,
    ln1_gain,
    ln1_bias,
    w_qkv,
    b_qkv,
    w_out,
    ln2_gain,
    ln2_bias,
    w_gate,
    w_up,
    w_down,
    cotangent,
):
    tokens = hidden_in[0].astype(F32)
    count, width = tokens.shape
    size = lax.axis_size("seq")
    length = count * size
    unit = width // size
    language_ids = jnp.arange(LANGS, dtype=jnp.int32)
    marks_all = (languages[:, None] == language_ids[None, :]).astype(jnp.int32)
    language_totals = jnp.sum(marks_all, 0)
    own_language = lax.dynamic_slice_in_dim(languages, lax.axis_index("row"), 1, 0)
    own_marks = (own_language[0] == language_ids).astype(jnp.int32)
    own_count = jnp.sum(own_marks * language_totals)
    row_weight = F32(languages.shape[0] * length) / (LANGS * (own_count * length).astype(F32))
    gain_one, shift_one = ln1_gain.astype(F32), ln1_bias.astype(F32)
    gain_two, shift_two = ln2_gain.astype(F32), ln2_bias.astype(F32)

    normed_one, inverse_one = standardize(tokens)
    first_in = (normed_one * gain_one + shift_one).astype(BF16)
    bias_rows = jnp.broadcast_to(b_qkv[None], (BIAS_ROWS,) + b_qkv.shape)
    moved = to_heads(jnp.concatenate(own_chunks(w_qkv) + [bias_rows], 0))
    flows = len(flows_of())
    heads_b = jnp.concatenate([part[-1:] for part in moved], 0)[None].astype(F32)
    moved = jnp.concatenate([part[:-BIAS_ROWS] for part in moved], -1)
    heads_w = row_gather(jnp.split(moved, flows, 0), BF16)
    places = gather_places(positions[0])
    tables = rotary_tables(places)
    first_full = lax.all_gather(first_in, "seq", axis=0, tiled=True)
    projected = mm(first_full, heads_w)
    parts = [projected[None, :, i * unit : (i + 1) * unit] for i in range(3)]
    mixed, *rotated, stats = attend(parts, heads_b, tables)
    mixed = mixed[0]
    middle = tokens + scatter_tokens(
        lambda row: mm(rows_of(mixed, row, CORES * count), w_out), count
    )

    normed_two, inverse_two = standardize(middle)
    second_in = (normed_two * gain_two + shift_two).astype(BF16)
    grad_top = cotangent[0].astype(F32) * row_weight
    grad_top_full = lax.all_gather(grad_top.astype(BF16), "seq", axis=0, tiled=True)
    second_full = gather_tokens(second_in)
    gate = mm(second_full, w_gate)
    upward = mm(second_full, w_up)
    sigmoid_gate = jax.nn.sigmoid(gate)
    activated = gate * sigmoid_gate
    hidden = (activated * upward).astype(BF16)
    grad_hidden = mm(grad_top_full, w_down, ROWS_COLS)
    slope = sigmoid_gate * (1.0 + gate * (1.0 - sigmoid_gate))
    grad_gate = (grad_hidden * upward * slope).astype(BF16)
    grad_upward = (grad_hidden * activated).astype(BF16)
    feed_grads = (
        mm(second_full, grad_gate, COLS_COLS).astype(BF16),
        mm(second_full, grad_upward, COLS_COLS).astype(BF16),
        mm(hidden, grad_top_full, COLS_COLS).astype(BF16),
    )
    grad_second = scatter_tokens(
        lambda row: mm(rows_of(grad_gate, row, CORES * count), w_gate, ROWS_COLS)
        + mm(rows_of(grad_upward, row, CORES * count), w_up, ROWS_COLS),
        count,
        feed_grads,
    )
    feed_grads = lax.psum(feed_grads, "row")
    grad_middle = grad_top + norm_back(grad_second * gain_two, normed_two, inverse_two)
    grad_middle_full = gather_tokens(grad_middle.astype(BF16))
    grad_mixed = mm(grad_middle_full, w_out, ROWS_COLS).astype(BF16)
    grad_w_out = lax.psum(
        after(mm(mixed, grad_middle_full, COLS_COLS).astype(BF16), *feed_grads), "row"
    ).astype(F32)
    grad_parts = attend_back(rotated, grad_mixed[None], stats, tables)
    grad_projected = jnp.concatenate([part[0] for part in grad_parts], 1)
    grad_b = jnp.sum(grad_projected.astype(F32), 0)
    grad_w_qkv = row_scatter(mm(first_full, grad_projected, COLS_COLS).astype(BF16))
    grad_w_qkv = jnp.concatenate(grad_w_qkv, 0)
    grad_w_qkv = from_heads([grad_w_qkv[:, i * unit : (i + 1) * unit] for i in range(3)])
    grad_w_qkv = row_gather(jnp.split(grad_w_qkv, flows, 0), F32)
    grad_first = scatter_tokens(
        lambda row: mm(rows_of(grad_projected, row, CORES * count), heads_w, ROWS_COLS), count
    )
    feed_out = scatter_tokens(lambda row: mm(rows_of(hidden, row, CORES * count), w_down), count)
    output = (middle + feed_out).astype(BF16)[None]
    input_grad = (grad_middle + norm_back(grad_first * gain_one, normed_one, inverse_one)).astype(
        BF16
    )[None]

    def shards(vector):
        return vector.reshape(size, -1)

    early = small_sums(
        jnp.concatenate(
            [shards(jnp.sum(grad_second * normed_two, 0)), shards(jnp.sum(grad_second, 0))], 1
        )
    )
    late = small_sums(
        jnp.concatenate(
            [shards(jnp.sum(grad_first * normed_one, 0)), shards(jnp.sum(grad_first, 0))], 1
        )
    )
    for bit in row_bits():
        grad_b = grad_b + row_swap(grad_b, bit)
    grad_b = from_heads([grad_b[i * unit : (i + 1) * unit] for i in range(3)])
    return (
        output,
        input_grad,
        late[:unit],
        late[unit:],
        grad_w_qkv,
        grad_b,
        grad_w_out,
        early[:unit],
        early[unit:],
        feed_grads[0].astype(F32),
        feed_grads[1].astype(F32),
        feed_grads[2].astype(F32),
    )


def solution(mesh):
    placed = (
        P("row", "seq", None),
        P("row", "seq"),
        P(),
        P(),
        P(),
        P(None, "seq"),
        P("seq"),
        P("seq", None),
        P(),
        P(),
        P(None, "seq"),
        P(None, "seq"),
        P("seq", None),
        P("row", "seq", None),
    )
    return jax.shard_map(
        body,
        mesh=mesh,
        in_specs=placed,
        out_specs=(
            P("row", "seq", None),
            P("row", "seq", None),
            P("seq"),
            P("seq"),
            P(None, "seq"),
            P("seq"),
            P("seq", None),
            P("seq"),
            P("seq"),
            P(None, "seq"),
            P(None, "seq"),
            P("seq", None),
        ),
        check_vma=False,
    )
```

profile of v0, /device:TPU:0, one launch (start us, length us, event | category | flops | bytes accessed | tf_op | source)
XLA Modules:
  0.0 630.7 jit_solution(4159883606279566638)
XLA Ops:
  31.4 14.4 %collective-permute-done.2 = bf16[528,256]{1,0:T(8,128)(2,1)} collective-permute-done((bf16[528,256]{1,0:T(8,128)(2,1)}, bf16[528,256]{1,0:T(8,128)(2,1)}, u32[]{:S(2)}, u32[]{:S(2)}) %collective-permute-start.2) | collective-permute-done | bytes 270368 | tf_op jit(solution)/shard_map/ppermute | solution.py:207
  67.8 11.2 %collective-permute-done.6 = bf16[256,768]{1,0:T(8,128)(2,1)S(1)} collective-permute-done((bf16[256,768]{1,0:T(8,128)(2,1)S(1)}, bf16[256,768]{1,0:T(8,128)(2,1)S(1)}, u32[]{:S(2)}, u32[]{:S(2)}) %collective-permute-start.6) | collective-permute-done | bytes 393248 | tf_op jit(solution)/shard_map/ppermute | solution.py:140
  90.8 6.1 fusion.124
  98.6 11.8 %attend.1 = (bf16[1,1024,256]{2,1,0:T(8,128)(2,1)}, bf16[1,1024,256]{2,1,0:T(8,128)(2,1)}, bf16[1,1024,256]{2,1,0:T(8,128)(2,1)}, bf16[1,1024,256]{2,1,0:T(8,128)(2,1)}, f32[1,1024,256]{2,1,0:T(8,128)}) custom-call(f32[1,1024,256]{2,1,0:T(8,128)} %get-tuple-element.60.q_in, f32[1,1024,256]{2,1,0:T(8,128)} %get-tuple-element.59.k_in, ...), custom_call_target="tpu_custom_call" | custom-call | tf_op jit(solution)/shard_map/attend/pallas_call | solution.py:359
  118.6 7.7 %collective-permute-done.16 = bf16[64,2048]{1,0:T(8,128)(2,1)S(1)} collective-permute-done((bf16[64,2048]{1,0:T(8,128)(2,1)S(1)}, bf16[64,2048]{1,0:T(8,128)(2,1)S(1)}, u32[]{:S(2)}, u32[]{:S(2)}) %collective-permute-start.16) | collective-permute-done | bytes 262176 | tf_op jit(solution)/shard_map/ppermute | solution.py:61
  134.3 8.6 %collective-permute-done.17 = bf16[64,2048]{1,0:T(8,128)(2,1)S(1)} collective-permute-done((bf16[64,2048]{1,0:T(8,128)(2,1)S(1)}, bf16[64,2048]{1,0:T(8,128)(2,1)S(1)}, u32[]{:S(2)}, u32[]{:S(2)}) %collective-permute-start.17) | collective-permute-done | bytes 262176 | tf_op jit(solution)/shard_map/ppermute | solution.py:61
  149.0 10.8 %collective-permute-done.18 = bf16[64,2048]{1,0:T(8,128)(2,1)} collective-permute-done((bf16[64,2048]{1,0:T(8,128)(2,1)}, bf16[64,2048]{1,0:T(8,128)(2,1)}, u32[]{:S(2)}, u32[]{:S(2)}) %collective-permute-start.18) | collective-permute-done | bytes 262176 | tf_op jit(solution)/shard_map/ppermute | solution.py:61
  171.1 5.9 fusion.126
  220.1 6.8 %multiply_convert_fusion = (bf16[1024,704]{0,1:T(8,128)(2,1)S(1)}, bf16[1024,704]{0,1:T(8,128)(2,1)S(1)}, bf16[1024,704]{0,1:T(8,128)(2,1)S(1)}) fusion(f32[1024,704]{0,1:T(8,128)S(1)} %fusion.126, f32[1024,704]{0,1:T(8,128)S(1)} %fusion.125, bf16[1024,2048]{1,0:T(8,128)(2,1)} %constant_dynamic-update-slice_fusion.16, bf16[2048,704]{0,1:T(8,128)(2,1)S(1)} %copy-done), kind=kOutput, calls=%fused_computation.5 | convolution fusion | flops 2963603456 | bytes 17170432 | tf_op jit(solution)/shard_map/dot_general | solution.py:42
  238.7 6.6 %convolution_convert_fusion.2 = bf16[2048,704]{0,1:T(8,128)(2,1)} fusion(bf16[1024,704]{0,1:T(8,128)(2,1)S(1)} %get-tuple-element.54, bf16[1024,2048]{1,0:T(8,128)(2,1)} %constant_dynamic-update-slice_fusion.16), kind=kOutput, calls=%fused_computation.2 | convolution fusion | flops 2954231808 | bytes 8519680 | tf_op jit(solution)/shard_map/dot_general | solution.py:42
  245.3 6.8 %convolution_convert_fusion.1 = bf16[2048,704]{0,1:T(8,128)(2,1)} fusion(bf16[1024,704]{0,1:T(8,128)(2,1)S(1)} %get-tuple-element.53, bf16[1024,2048]{1,0:T(8,128)(2,1)} %constant_dynamic-update-slice_fusion.16), kind=kOutput, calls=%fused_computation.1 | convolution fusion | flops 2954231808 | bytes 8519680 | tf_op jit(solution)/shard_map/dot_general | solution.py:42
  289.9 9.0 %collective-permute-done.58 = bf16[64,2048]{1,0:T(8,128)(2,1)S(1)} collective-permute-done((bf16[64,2048]{1,0:T(8,128)(2,1)S(1)}, bf16[64,2048]{1,0:T(8,128)(2,1)S(1)}, u32[]{:S(2)}, u32[]{:S(2)}) %collective-permute-start.58) | collective-permute-done | bytes 262176 | tf_op jit(solution)/shard_map/ppermute | solution.py:61
  310.1 5.6 collective-permute-done.51
  321.3 5.6 collective-permute-done.66
  332.6 5.6 collective-permute-done.52
  350.2 10.0 %collective-permute-done.119 = f32[4,512]{1,0:T(4,128)S(1)} collective-permute-done((f32[4,512]{1,0:T(4,128)S(1)}, f32[4,512]{1,0:T(4,128)S(1)}, u32[]{:S(2)}, u32[]{:S(2)}) %collective-permute-start.119) | collective-permute-done | bytes 8224 | tf_op jit(solution)/shard_map/ppermute | solution.py:241
  381.6 5.7 collective-permute-done.74
  407.6 14.8 %attend_back.1 = (bf16[1,1024,256]{2,1,0:T(8,128)(2,1)}, bf16[1,1024,256]{2,1,0:T(8,128)(2,1)}, bf16[1,1024,256]{2,1,0:T(8,128)(2,1)}) custom-call(bf16[1,1024,256]{2,1,0:T(8,128)(2,1)} %get-tuple-element.24.q_in, bf16[1,1024,256]{2,1,0:T(8,128)(2,1)} %get-tuple-element.25.k_in, bf16[1,1024,256]{2,1,0:T(8,128)(2,1)} %get-tuple-element.26.v_in, ...), custom_call_target="tpu_custom_call" | custom-call | tf_op jit(solution)/shard_map/attend_back/pallas_call | solution.py:376
  448.0 6.2 convolution_convert_fusion
  464.8 8.1 %collective-permute-done.86 = bf16[64,2048]{1,0:T(8,128)(2,1)S(1)} collective-permute-done((bf16[64,2048]{1,0:T(8,128)(2,1)S(1)}, bf16[64,2048]{1,0:T(8,128)(2,1)S(1)}, u32[]{:S(2)}, u32[]{:S(2)}) %collective-permute-start.86) | collective-permute-done | bytes 262176 | tf_op jit(solution)/shard_map/ppermute | solution.py:61
  485.1 6.4 %collective-permute-done.87 = bf16[64,2048]{1,0:T(8,128)(2,1)S(1)} collective-permute-done((bf16[64,2048]{1,0:T(8,128)(2,1)S(1)}, bf16[64,2048]{1,0:T(8,128)(2,1)S(1)}, u32[]{:S(2)}, u32[]{:S(2)}) %collective-permute-start.87) | collective-permute-done | bytes 262176 | tf_op jit(solution)/shard_map/ppermute | solution.py:61
  556.2 6.2 collective-permute-done.109
  563.4 7.6 %collective-permute-done.110 = bf16[256,768]{1,0:T(8,128)(2,1)} collective-permute-done((bf16[256,768]{1,0:T(8,128)(2,1)S(1)}, bf16[256,768]{1,0:T(8,128)(2,1)}, u32[]{:S(2)}, u32[]{:S(2)}) %collective-permute-start.110) | collective-permute-done | bytes 393248 | tf_op jit(solution)/shard_map/ppermute | solution.py:140
  586.5 34.7 %all-reduce.4.cloned.1.call-done = bf16[256,2048]{1,0:T(8,128)(2,1)} async-done(((bf16[256,2048]{1,0:T(8,128)(2,1)}), bf16[256,2048]{1,0:T(8,128)(2,1)}) %all-reduce.4.cloned.1.call-update) | async-done | bytes 1048592 | tf_op jit(solution)/shard_map/psum | solution.py:466
  (578 shorter events, 391.3 us)
Async XLA Ops:
  7.2 83.6 %all-gather.3.cloned.1.call-start = ((), (), s32[]{:S(2)}) async-start(), calls=%async_computation | async-start | bytes 4718592 | tf_op jit(solution)/shard_map/all_gather | solution.py:428
  13.6 157.5 %all-gather.5.cloned.1.call-start = ((), (), s32[]{:S(2)}) async-start(), calls=%async_computation.1 | async-start | bytes 4718592 | tf_op jit(solution)/shard_map/all_gather | solution.py:440
  15.9 29.8 %collective-permute-start.2 = (bf16[528,256]{1,0:T(8,128)(2,1)}, bf16[528,256]{1,0:T(8,128)(2,1)}, u32[]{:S(2)}, u32[]{:S(2)}) collective-permute-start(bf16[528,256]{1,0:T(8,128)(2,1)} %get-tuple-element.134), channel_id=1, source_target_pairs={{0,2},{1,5},{2,0},{3,3},{4,6},{5,1},{6,4},{7,7},{8,10},{9,13},{10,... | collective-permute-start | bytes 811016 | tf_op jit(solution)/shard_map/ppermute | solution.py:207
  20.9 24.9 %collective-permute-start.1 = (bf16[528,256]{1,0:T(8,128)(2,1)}, bf16[528,256]{1,0:T(8,128)(2,1)}, u32[]{:S(2)}, u32[]{:S(2)}) collective-permute-start(bf16[528,256]{1,0:T(8,128)(2,1)} %get-tuple-element.135), channel_id=1, source_target_pairs={{0,1},{1,4},{2,7},{3,2},{4,5},{5,0},{6,3},{7,6},{8,9},{9,12},{10,1... | collective-permute-start | bytes 811016 | tf_op jit(solution)/shard_map/ppermute | solution.py:207
  21.5 24.3 %collective-permute-start = (bf16[528,256]{1,0:T(8,128)(2,1)}, bf16[528,256]{1,0:T(8,128)(2,1)}, u32[]{:S(2)}, u32[]{:S(2)}) collective-permute-start(bf16[528,256]{1,0:T(8,128)(2,1)} %get-tuple-element.133), channel_id=1, source_target_pairs={{0,0},{1,3},{2,6},{3,1},{4,4},{5,7},{6,2},{7,5},{8,8},{9,11},{10,1... | collective-permute-start | bytes 811016 | tf_op jit(solution)/shard_map/ppermute | solution.py:207
  29.2 534.2 %all-reduce.6.cloned.1.call-start = ((), (), s32[]{:S(2)}) async-start(), calls=%async_computation.3 | async-start | bytes 17301504 | tf_op jit(solution)/shard_map/psum | solution.py:462
  29.6 23.8 %collective-permute-start.10 = (s32[256]{0:T(256)S(1)}, s32[256]{0:T(256)S(1)}, u32[]{:S(2)}, u32[]{:S(2)}) collective-permute-start(s32[256]{0:T(256)S(1)} %add_select_fusion.2), channel_id=1, source_target_pairs={{0,2},{1,3},{2,0},{3,1},{4,6},{5,7},{6,4},{7,5},{8,10},{9,11},{10,... | collective-permute-start | bytes 3080 | tf_op jit(solution)/shard_map/ppermute | solution.py:78
  58.3 23.9 %collective-permute-start.4 = (bf16[256,768]{1,0:T(8,128)(2,1)}, bf16[256,768]{1,0:T(8,128)(2,1)S(1)}, u32[]{:S(2)}, u32[]{:S(2)}) collective-permute-start(bf16[256,768]{1,0:T(8,128)(2,1)} %get-tuple-element.146), channel_id=1, source_target_pairs={{0,8},{8,0},{16,24},{24,16},{1,9},{9,1},{17,25},{25,17},{2,10},{10... | collective-permute-start | bytes 1179656 | tf_op jit(solution)/shard_map/ppermute | solution.py:140
  63.4 25.8 %collective-permute-start.7 = (bf16[256,768]{1,0:T(8,128)(2,1)S(1)}, bf16[256,768]{1,0:T(8,128)(2,1)S(1)}, u32[]{:S(2)}, u32[]{:S(2)}) collective-permute-start(bf16[256,768]{1,0:T(8,128)(2,1)S(1)} %get-tuple-element.144), channel_id=1, source_target_pairs={{0,16},{8,24},{16,0},{24,8},{1,17},{9,25},{17,1},{25,9},{2,18},{10... | collective-permute-start | bytes 1179656 | tf_op jit(solution)/shard_map/ppermute | solution.py:140
  64.8 22.1 %collective-permute-start.5 = (bf16[256,768]{1,0:T(8,128)(2,1)}, bf16[256,768]{1,0:T(8,128)(2,1)S(1)}, u32[]{:S(2)}, u32[]{:S(2)}) collective-permute-start(bf16[256,768]{1,0:T(8,128)(2,1)} %collective-permute-done.3), channel_id=1, source_target_pairs={{0,8},{8,0},{16,24},{24,16},{1,9},{9,1},{17,25},{25,17},{2,10},{10... | collective-permute-start | bytes 1179656 | tf_op jit(solution)/shard_map/ppermute | solution.py:140
  263.5 357.7 %all-reduce.4.cloned.1.call-start = ((), (), s32[]{:S(2)}) async-start(), calls=%async_computation.2 | async-start | bytes 2097152 | tf_op jit(solution)/shard_map/psum | solution.py:466
  265.8 22.0 %collective-permute-start.43 = (bf16[64,2048]{1,0:T(8,128)(2,1)}, bf16[64,2048]{1,0:T(8,128)(2,1)}, u32[]{:S(2)}, u32[]{:S(2)}) collective-permute-start(bf16[64,2048]{1,0:T(8,128)(2,1)} %get-tuple-element.109), channel_id=1, source_target_pairs={{0,1},{1,0},{2,3},{3,2},{4,5},{5,4},{6,7},{7,6},{8,9},{9,8},{10,11... | collective-permute-start | bytes 786440 | tf_op jit(solution)/shard_map/ppermute | solution.py:55
  268.6 36.1 %collective-permute-start.42 = (bf16[64,2048]{1,0:T(8,128)(2,1)}, bf16[64,2048]{1,0:T(8,128)(2,1)}, u32[]{:S(2)}, u32[]{:S(2)}) collective-permute-start(bf16[64,2048]{1,0:T(8,128)(2,1)} %get-tuple-element.105), channel_id=1, source_target_pairs={{0,1},{1,0},{2,3},{3,2},{4,5},{5,4},{6,7},{7,6},{8,9},{9,8},{10,11... | collective-permute-start | bytes 786440 | tf_op jit(solution)/shard_map/ppermute | solution.py:55
  289.5 37.6 %collective-permute-start.41 = (bf16[64,2048]{1,0:T(8,128)(2,1)S(1)}, bf16[64,2048]{1,0:T(8,128)(2,1)S(1)}, u32[]{:S(2)}, u32[]{:S(2)}) collective-permute-start(bf16[64,2048]{1,0:T(8,128)(2,1)S(1)} %copy-done.54), channel_id=1, source_target_pairs={{0,1},{1,0},{2,3},{3,2},{4,5},{5,4},{6,7},{7,6},{8,9},{9,8},{10,11... | collective-permute-start | bytes 786440 | tf_op jit(solution)/shard_map/ppermute | solution.py:55
  317.0 48.4 %collective-permute-start.40 = (bf16[64,2048]{1,0:T(8,128)(2,1)}, bf16[64,2048]{1,0:T(8,128)(2,1)}, u32[]{:S(2)}, u32[]{:S(2)}) collective-permute-start(bf16[64,2048]{1,0:T(8,128)(2,1)} %get-tuple-element.97), channel_id=1, source_target_pairs={{0,1},{1,0},{2,3},{3,2},{4,5},{5,4},{6,7},{7,6},{8,9},{9,8},{10,11... | collective-permute-start | bytes 786440 | tf_op jit(solution)/shard_map/ppermute | solution.py:55
  339.2 26.7 %collective-permute-start.47 = (bf16[64,2048]{1,0:T(8,128)(2,1)S(1)}, bf16[64,2048]{1,0:T(8,128)(2,1)}, u32[]{:S(2)}, u32[]{:S(2)}) collective-permute-start(bf16[64,2048]{1,0:T(8,128)(2,1)S(1)} %copy-done.52), channel_id=1, source_target_pairs={{0,1},{1,0},{2,3},{3,2},{4,5},{5,4},{6,7},{7,6},{8,9},{9,8},{10,11... | collective-permute-start | bytes 786440 | tf_op jit(solution)/shard_map/ppermute | solution.py:55
  339.3 26.7 %collective-permute-start.46 = (bf16[64,2048]{1,0:T(8,128)(2,1)}, bf16[64,2048]{1,0:T(8,128)(2,1)}, u32[]{:S(2)}, u32[]{:S(2)}) collective-permute-start(bf16[64,2048]{1,0:T(8,128)(2,1)} %get-tuple-element.99), channel_id=1, source_target_pairs={{0,2},{1,3},{2,4},{3,5},{4,6},{5,7},{6,0},{7,1},{8,10},{9,11},{10,... | collective-permute-start | bytes 786440 | tf_op jit(solution)/shard_map/ppermute | solution.py:61
  343.8 22.5 %collective-permute-start.53 = (bf16[64,2048]{1,0:T(8,128)(2,1)}, bf16[64,2048]{1,0:T(8,128)(2,1)}, u32[]{:S(2)}, u32[]{:S(2)}) collective-permute-start(bf16[64,2048]{1,0:T(8,128)(2,1)} %get-tuple-element.100), channel_id=1, source_target_pairs={{0,2},{1,3},{2,4},{3,5},{4,6},{5,7},{6,0},{7,1},{8,10},{9,11},{10,... | collective-permute-start | bytes 786440 | tf_op jit(solution)/shard_map/ppermute | solution.py:61
  461.7 22.8 %collective-permute-start.83 = (bf16[64,2048]{1,0:T(8,128)(2,1)S(1)}, bf16[64,2048]{1,0:T(8,128)(2,1)S(1)}, u32[]{:S(2)}, u32[]{:S(2)}) collective-permute-start(bf16[64,2048]{1,0:T(8,128)(2,1)S(1)} %get-tuple-element.69), channel_id=1, source_target_pairs={{0,1},{1,0},{2,3},{3,2},{4,5},{5,4},{6,7},{7,6},{8,9},{9,8},{10,11... | collective-permute-start | bytes 786440 | tf_op jit(solution)/shard_map/ppermute | solution.py:55
  462.2 22.3 %collective-permute-start.90 = (bf16[64,2048]{1,0:T(8,128)(2,1)S(1)}, bf16[64,2048]{1,0:T(8,128)(2,1)S(1)}, u32[]{:S(2)}, u32[]{:S(2)}) collective-permute-start(bf16[64,2048]{1,0:T(8,128)(2,1)S(1)} %get-tuple-element.70), channel_id=1, source_target_pairs={{0,1},{1,0},{2,3},{3,2},{4,5},{5,4},{6,7},{7,6},{8,9},{9,8},{10,11... | collective-permute-start | bytes 786440 | tf_op jit(solution)/shard_map/ppermute | solution.py:55
  491.4 21.7 %collective-permute-start.103 = (bf16[512,768]{1,0:T(8,128)(2,1)}, bf16[512,768]{1,0:T(8,128)(2,1)}, u32[]{:S(2)}, u32[]{:S(2)}) collective-permute-start(bf16[512,768]{1,0:T(8,128)(2,1)} %constant_dynamic-slice_fusion.10), channel_id=1, source_target_pairs={{0,16},{8,24},{16,0},{24,8},{1,17},{9,25},{17,1},{25,9},{2,18},{10... | collective-permute-start | bytes 2359304 | tf_op jit(solution)/shard_map/ppermute | solution.py:140
  501.8 27.1 %collective-permute-start.102 = (bf16[256,768]{1,0:T(8,128)(2,1)}, bf16[256,768]{1,0:T(8,128)(2,1)}, u32[]{:S(2)}, u32[]{:S(2)}) collective-permute-start(bf16[256,768]{1,0:T(8,128)(2,1)} %constant_dynamic-slice_fusion.11), channel_id=1, source_target_pairs={{0,16},{8,24},{16,0},{24,8},{1,17},{9,25},{17,1},{25,9},{2,18},{10... | collective-permute-start | bytes 1179656 | tf_op jit(solution)/shard_map/ppermute | solution.py:140
  546.8 28.0 %collective-permute-start.112 = (bf16[256,768]{1,0:T(8,128)(2,1)S(1)}, bf16[256,768]{1,0:T(8,128)(2,1)S(1)}, u32[]{:S(2)}, u32[]{:S(2)}) collective-permute-start(bf16[256,768]{1,0:T(8,128)(2,1)S(1)} %get-tuple-element.136), channel_id=1, source_target_pairs={{0,16},{8,24},{16,0},{24,8},{1,17},{9,25},{17,1},{25,9},{2,18},{10... | collective-permute-start | bytes 1179656 | tf_op jit(solution)/shard_map/ppermute | solution.py:140
  554.0 21.7 %collective-permute-start.113 = (bf16[256,768]{1,0:T(8,128)(2,1)S(1)}, bf16[256,768]{1,0:T(8,128)(2,1)S(1)}, u32[]{:S(2)}, u32[]{:S(2)}) collective-permute-start(bf16[256,768]{1,0:T(8,128)(2,1)S(1)} %collective-permute-done.111), channel_id=1, source_target_pairs={{0,16},{8,24},{16,0},{24,8},{1,17},{9,25},{17,1},{25,9},{2,18},{10... | collective-permute-start | bytes 1179656 | tf_op jit(solution)/shard_map/ppermute | solution.py:140
  (166 other events, 2069.1 us)
Sparse Core Ops, SparseCore 0:
  13.7 55.8 all-gather.2
  71.8 49.5 all-gather.4
  263.6 173.8 all-reduce.5
  563.5 57.6 all-reduce.3
where the time goes:
time: 640 us; the launch traced here: 631 us
  waiting for transfers between devices  300 us (47%)
  matrix products  100 us (16%)
  starting transfers between devices  69.3 us (11%)
  local copies, waits for them, and re-layouts  59.5 us (9%)
  other arithmetic  58.1 us (9%)
  Pallas kernels  26.6 us (4%)
  between operations  17.2 us (3%)
    ppermute x36, waiting for transfers between devices, ring(): return [lax.ppermute(part, 'seq', to) for part in value]  181 us
    dot_general x30, matrix products, mm(): lax.dot_general(left, right, (dims, ((), ())), preferred_element_type=F32)  100 us
    ppermute x22, waiting for transfers between devices, row_swap(): return lax.ppermute(value, 'row', [(d, d ^ bit) for d in range(size)])  42.8 us
    psum x1, waiting for transfers between devices, body(): lax.psum(after(mm(mixed, grad_middle_full, COLS_COLS).astype(BF16), *feed...  34.7 us
    ppermute x22, starting transfers between devices, row_swap(): return lax.ppermute(value, 'row', [(d, d ^ bit) for d in range(size)])  27.9 us
    ppermute x6, waiting for transfers between devices, small_sums(): lax.ppermute(pick(halves, 1 - own), 'seq', [(d, d ^ bit) for d in range(s...  18.2 us
    pallas_call x1, Pallas kernels, attend_back(): pl.pallas_call(attend_back_kernel, grid=(width // LANES,), in_specs=[spec...  14.8 us
    ppermute x3, waiting for transfers between devices, to_heads(): lax.ppermute(units[..., i * unit:(i + 1) * unit], 'seq', [(d, (3 * d + i)...  14.4 us
  transfers between devices with their start and end apart: 128, of which 58 were waited for; matrix products, arithmetic and copies ran while one was open for 24% of the time, Pallas kernels for 4%

commit v1 on v0

--- a/solution.py
+++ b/solution.py
@@ -93,7 +93,9 @@
     full = jnp.zeros((size * count,) + local.shape[1:], local.dtype)
     piece = cut(local)
     for step in range(chips):
-        following = ring(piece) if step + 1 < chips else None
+        following = None
+        if step + 1 < chips:
+            following = ring(piece)
         base = ((chip - step) % chips) * CORES
         rows = count // SPLITS
         for k, part in enumerate(piece):
@@ -171,20 +173,24 @@
     return done
 
 
-def row_gather(chunks, dtype):
-    flows = flows_of()
-    rows, columns = chunks[0].shape
+def row_pieces(chunks):
+    rows = chunks[0].shape[0]
     total = rows * lax.axis_size("row")
-    full = jnp.zeros((total * len(flows), columns), dtype)
-    for number, order in enumerate(flows):
+    found = []
+    for number, order in enumerate(flows_of()):
         pieces = [(place_in(order), chunks[number])]
         for level, bit in enumerate(reversed(order)):
             flip = (1 - 2 * side(bit)) << level
             pieces = pieces + [(at + flip, row_swap(piece, bit)) for at, piece in pieces]
-        for at, piece in pieces:
-            full = lax.dynamic_update_slice_in_dim(
-                full, piece.astype(dtype), number * total + at * rows, 0
-            )
+        found += [(number * total + at * rows, piece) for at, piece in pieces]
+    return found
+
+
+def row_gather(chunks):
+    pieces = row_pieces(chunks)
+    full = jnp.zeros((chunks[0].shape[0] * len(pieces), chunks[0].shape[1]), chunks[0].dtype)
+    for start, piece in pieces:
+        full = lax.dynamic_update_slice_in_dim(full, piece, start, 0)
     return full
 
 
@@ -384,6 +390,32 @@
     )(*rotated, grad, stats, *tables)
 
 
+def assemble_kernel(starts, *refs):
+    pieces, left, right = refs[:-2], refs[-2], refs[-1]
+    columns = left.shape[1]
+    for number, piece in enumerate(pieces):
+        rows = piece.shape[0]
+        start = pl.multiple_of(starts[number], rows)
+        left[pl.ds(start, rows), :] = piece[:, :columns].astype(F32)
+        right[:, pl.ds(start, rows)] = piece[:, columns:].astype(F32).T
+
+
+def assemble(pieces, columns):
+    rows, total = pieces[0][1].shape
+    length = rows * len(pieces)
+    vmem = pl.BlockSpec(memory_space=pltpu.VMEM)
+    return pl.pallas_call(
+        assemble_kernel,
+        in_specs=[pl.BlockSpec(memory_space=pltpu.SMEM)] + [vmem] * len(pieces),
+        out_specs=[vmem, vmem],
+        out_shape=[
+            jax.ShapeDtypeStruct((length, columns), F32),
+            jax.ShapeDtypeStruct((total - columns, length), F32),
+        ],
+        name="assemble",
+    )(jnp.stack([start for start, _ in pieces]).astype(jnp.int32), *[piece for _, piece in pieces])
+
+
 def body(
     hidden_in,
     positions,
@@ -422,7 +454,7 @@
     flows = len(flows_of())
     heads_b = jnp.concatenate([part[-1:] for part in moved], 0)[None].astype(F32)
     moved = jnp.concatenate([part[:-BIAS_ROWS] for part in moved], -1)
-    heads_w = row_gather(jnp.split(moved, flows, 0), BF16)
+    heads_w = row_gather(jnp.split(moved, flows, 0))
     places = gather_places(positions[0])
     tables = rotary_tables(places)
     first_full = lax.all_gather(first_in, "seq", axis=0, tiled=True)
@@ -462,22 +494,24 @@
     feed_grads = lax.psum(feed_grads, "row")
     grad_middle = grad_top + norm_back(grad_second * gain_two, normed_two, inverse_two)
     grad_middle_full = gather_tokens(grad_middle.astype(BF16))
+    feed_out = scatter_tokens(lambda row: mm(rows_of(hidden, row, CORES * count), w_down), count)
     grad_mixed = mm(grad_middle_full, w_out, ROWS_COLS).astype(BF16)
-    grad_w_out = lax.psum(
-        after(mm(mixed, grad_middle_full, COLS_COLS).astype(BF16), *feed_grads), "row"
-    ).astype(F32)
     grad_parts = attend_back(rotated, grad_mixed[None], stats, tables)
     grad_projected = jnp.concatenate([part[0] for part in grad_parts], 1)
     grad_b = jnp.sum(grad_projected.astype(F32), 0)
-    grad_w_qkv = row_scatter(mm(first_full, grad_projected, COLS_COLS).astype(BF16))
-    grad_w_qkv = jnp.concatenate(grad_w_qkv, 0)
-    grad_w_qkv = from_heads([grad_w_qkv[:, i * unit : (i + 1) * unit] for i in range(3)])
-    grad_w_qkv = row_gather(jnp.split(grad_w_qkv, flows, 0), F32)
+    grad_w_out = mm(grad_middle_full, mixed, COLS_COLS).astype(BF16)
+    grad_w_qkv = mm(first_full, grad_projected, COLS_COLS).astype(BF16)
+    attn_grads = jnp.concatenate([grad_w_qkv, grad_w_out], 1)
+    attn_grads = jnp.concatenate(row_scatter(attn_grads), 0)
+    back = from_heads([attn_grads[:, i * unit : (i + 1) * unit] for i in range(3)])
+    attn_grads = jnp.concatenate([back, attn_grads[:, 3 * unit :]], 1)
+    pieces = row_pieces(jnp.split(attn_grads, flows, 0))
+    grad_w_qkv, grad_w_out = assemble(pieces, 3 * unit)
     grad_first = scatter_tokens(
         lambda row: mm(rows_of(grad_projected, row, CORES * count), heads_w, ROWS_COLS), count
     )
-    feed_out = scatter_tokens(lambda row: mm(rows_of(hidden, row, CORES * count), w_down), count)
     output = (middle + feed_out).astype(BF16)[None]
+    feed_grads = [part.astype(F32) for part in feed_grads]
     input_grad = (grad_middle + norm_back(grad_first * gain_one, normed_one, inverse_one)).astype(
         BF16
     )[None]
@@ -485,32 +519,31 @@
     def shards(vector):
         return vector.reshape(size, -1)
 
-    early = small_sums(
+    own = jnp.arange(size, dtype=jnp.int32)[None, :, None] == lax.axis_index("seq")
+    placed_b = jnp.where(own, grad_b.reshape(3, 1, unit), 0.0).reshape(size, 3 * unit)
+    sums = small_sums(
         jnp.concatenate(
-            [shards(jnp.sum(grad_second * normed_two, 0)), shards(jnp.sum(grad_second, 0))], 1
+            [
+                shards(jnp.sum(grad_first * normed_one, 0)),
+                shards(jnp.sum(grad_first, 0)),
+                shards(jnp.sum(grad_second * normed_two, 0)),
+                shards(jnp.sum(grad_second, 0)),
+                placed_b,
+            ],
+            1,
         )
     )
-    late = small_sums(
-        jnp.concatenate(
-            [shards(jnp.sum(grad_first * normed_one, 0)), shards(jnp.sum(grad_first, 0))], 1
-        )
-    )
-    for bit in row_bits():
-        grad_b = grad_b + row_swap(grad_b, bit)
-    grad_b = from_heads([grad_b[i * unit : (i + 1) * unit] for i in range(3)])
     return (
         output,
         input_grad,
-        late[:unit],
-        late[unit:],
+        sums[:unit],
+        sums[unit : 2 * unit],
         grad_w_qkv,
-        grad_b,
+        sums[4 * unit :],
         grad_w_out,
-        early[:unit],
-        early[unit:],
-        feed_grads[0].astype(F32),
-        feed_grads[1].astype(F32),
-        feed_grads[2].astype(F32),
+        sums[2 * unit : 3 * unit],
+        sums[3 * unit : 4 * unit],
+        *feed_grads,
     )
 
 

time: 640 us -> 607 us (0.948)
  waiting for transfers between devices: 300 us -> 259 us
  local copies, waits for them, and re-layouts: 59.5 us -> 75.1 us
  starting transfers between devices: 69.3 us -> 56.9 us
    psum x1 -> x0, waiting for transfers between devices: 34.7 us -> none  [body(): lax.psum(after(mm(mixed, grad_middle_full, COLS_COLS).astype(BF16), *feed...]
    ppermute x6 -> x3, waiting for transfers between devices: 18.2 us -> 0.01 us  [small_sums(): lax.ppermute(pick(halves, 1 - own), 'seq', [(d, d ^ bit) for d in range(s...]
    ppermute x22 -> x18, waiting for transfers between devices: 42.8 us -> 59.3 us  [row_swap(): return lax.ppermute(value, 'row', [(d, d ^ bit) for d in range(size)])]
    dynamic_update_slice x8 -> x0, other arithmetic: 8.44 us -> none  [row_gather(): lax.dynamic_update_slice_in_dim(full, piece.astype(dtype), number * total...]
    ppermute x36, waiting for transfers between devices: 181 us -> 173 us  [ring(): return [lax.ppermute(part, 'seq', to) for part in value]]
    ppermute x6 -> x3, starting transfers between devices: 10.1 us -> 3.35 us  [from_heads(): lax.ppermute(pick(stacked, part), 'seq', [((3 * d + i) % size, d) for d i...]
    dynamic_update_slice x16, local copies, waits for them, and re-layouts: 6.91 us -> 13.4 us  [gather_tokens(): lax.dynamic_update_slice_in_dim(full, other, (base + 1 - core) * count +...]
    ppermute x22 -> x18, starting transfers between devices: 27.9 us -> 22.7 us  [row_swap(): return lax.ppermute(value, 'row', [(d, d ^ bit) for d in range(size)])]
  transfers between devices with their start and end apart: 128 -> 117, of which waited for: 58 -> 49; matrix products, arithmetic and copies ran while one was open for 24% -> 26% of each run, Pallas kernels for 4% -> 6%
where the time goes in v1:
time: 607 us; the launch traced here: 597 us
  waiting for transfers between devices  259 us (43%)
  matrix products  99.7 us (16%)
  local copies, waits for them, and re-layouts  75.1 us (12%)
  starting transfers between devices  56.9 us (9%)
  other arithmetic  56.4 us (9%)
  Pallas kernels  32.9 us (5%)
  between operations  17 us (3%)
    ppermute x36, waiting for transfers between devices, ring(): return [lax.ppermute(part, 'seq', to) for part in value]  173 us
    dot_general x30, matrix products, mm(): lax.dot_general(left, right, (dims, ((), ())), preferred_element_type=F32)  99.7 us
    ppermute x18, waiting for transfers between devices, row_swap(): return lax.ppermute(value, 'row', [(d, d ^ bit) for d in range(size)])  59.3 us
    ppermute x18, starting transfers between devices, row_swap(): return lax.ppermute(value, 'row', [(d, d ^ bit) for d in range(size)])  22.7 us
    pallas_call x1, Pallas kernels, attend_back(): pl.pallas_call(attend_back_kernel, grid=(width // LANES,), in_specs=[spec...  15 us
    ppermute x3, waiting for transfers between devices, to_heads(): lax.ppermute(units[..., i * unit:(i + 1) * unit], 'seq', [(d, (3 * d + i)...  14.4 us
    convert_element_type x16, local copies, waits for them, and re-layouts, scatter_tokens(): rows_of(block, (1 - core) * count + k * rows, rows).astype(BF16)  14.1 us
    dynamic_update_slice x16, local copies, waits for them, and re-layouts, gather_tokens(): lax.dynamic_update_slice_in_dim(full, other, (base + 1 - core) * count +...  13.4 us
  transfers between devices with their start and end apart: 117, of which 49 were waited for; matrix products, arithmetic and copies ran while one was open for 26% of the time, Pallas kernels for 6%

profile of v1, /device:TPU:0, one launch (start us, length us, event | category | flops | bytes accessed | tf_op | source)
XLA Modules:
  0.0 596.9 jit_solution(3912667473282263805)
XLA Ops:
  31.4 14.4 %collective-permute-done.2 = bf16[528,256]{1,0:T(8,128)(2,1)} collective-permute-done((bf16[528,256]{1,0:T(8,128)(2,1)}, bf16[528,256]{1,0:T(8,128)(2,1)}, u32[]{:S(2)}, u32[]{:S(2)}) %collective-permute-start.2) | collective-permute-done | bytes 270368 | tf_op jit(solution)/shard_map/ppermute | solution.py:213
  67.8 11.2 %collective-permute-done.6 = bf16[256,768]{1,0:T(8,128)(2,1)S(1)} collective-permute-done((bf16[256,768]{1,0:T(8,128)(2,1)S(1)}, bf16[256,768]{1,0:T(8,128)(2,1)S(1)}, u32[]{:S(2)}, u32[]{:S(2)}) %collective-permute-start.6) | collective-permute-done | bytes 393248 | tf_op jit(solution)/shard_map/ppermute | solution.py:142
  90.8 6.1 %fusion.123 = f32[1024,768]{1,0:T(8,128)S(1)} fusion(bf16[1024,2048]{1,0:T(8,128)(2,1)} %all-gather.3.cloned.1.call-done, bf16[2048,768]{1,0:T(8,128)(2,1)} %constant_dynamic-update-slice_fusion.32), kind=kOutput, calls=%fused_computation.331 | convolution fusion | flops 3221225472 | bytes 10485760 | tf_op jit(solution)/shard_map/dot_general | solution.py:42
  98.6 11.8 %attend.1 = (bf16[1,1024,256]{2,1,0:T(8,128)(2,1)}, bf16[1,1024,256]{2,1,0:T(8,128)(2,1)}, bf16[1,1024,256]{2,1,0:T(8,128)(2,1)}, bf16[1,1024,256]{2,1,0:T(8,128)(2,1)}, f32[1,1024,256]{2,1,0:T(8,128)}) custom-call(f32[1,1024,256]{2,1,0:T(8,128)} %get-tuple-element.60.q_in, f32[1,1024,256]{2,1,0:T(8,128)} %get-tuple-element.59.k_in, ...), custom_call_target="tpu_custom_call" | custom-call | tf_op jit(solution)/shard_map/attend/pallas_call | solution.py:365
  118.6 7.7 %collective-permute-done.16 = bf16[64,2048]{1,0:T(8,128)(2,1)S(1)} collective-permute-done((bf16[64,2048]{1,0:T(8,128)(2,1)S(1)}, bf16[64,2048]{1,0:T(8,128)(2,1)S(1)}, u32[]{:S(2)}, u32[]{:S(2)}) %collective-permute-start.16) | collective-permute-done | bytes 262176 | tf_op jit(solution)/shard_map/ppermute | solution.py:61
  134.3 8.6 %collective-permute-done.17 = bf16[64,2048]{1,0:T(8,128)(2,1)S(1)} collective-permute-done((bf16[64,2048]{1,0:T(8,128)(2,1)S(1)}, bf16[64,2048]{1,0:T(8,128)(2,1)S(1)}, u32[]{:S(2)}, u32[]{:S(2)}) %collective-permute-start.17) | collective-permute-done | bytes 262176 | tf_op jit(solution)/shard_map/ppermute | solution.py:61
  149.6 10.2 %collective-permute-done.18 = bf16[64,2048]{1,0:T(8,128)(2,1)} collective-permute-done((bf16[64,2048]{1,0:T(8,128)(2,1)}, bf16[64,2048]{1,0:T(8,128)(2,1)}, u32[]{:S(2)}, u32[]{:S(2)}) %collective-permute-start.18) | collective-permute-done | bytes 262176 | tf_op jit(solution)/shard_map/ppermute | solution.py:61
  171.1 5.9 fusion.125
  220.1 6.8 %multiply_convert_fusion = (bf16[1024,704]{0,1:T(8,128)(2,1)S(1)}, bf16[1024,704]{0,1:T(8,128)(2,1)S(1)}, bf16[1024,704]{0,1:T(8,128)(2,1)S(1)}) fusion(f32[1024,704]{0,1:T(8,128)S(1)} %fusion.125, f32[1024,704]{0,1:T(8,128)S(1)} %fusion.124, bf16[1024,2048]{1,0:T(8,128)(2,1)} %constant_dynamic-update-slice_fusion.16, bf16[2048,704]{0,1:T(8,128)(2,1)S(1)} %copy-done), kind=kOutput, calls=%fused_computation.7 | convolution fusion | flops 2963603456 | bytes 17170432 | tf_op jit(solution)/shard_map/dot_general | solution.py:42
  238.7 6.6 %convolution_convert_fusion.2 = bf16[2048,704]{0,1:T(8,128)(2,1)} fusion(bf16[1024,704]{0,1:T(8,128)(2,1)S(1)} %get-tuple-element.56, bf16[1024,2048]{1,0:T(8,128)(2,1)} %constant_dynamic-update-slice_fusion.16), kind=kOutput, calls=%fused_computation.4 | convolution fusion | flops 2954231808 | bytes 8519680 | tf_op jit(solution)/shard_map/dot_general | solution.py:42
  245.4 6.8 %convolution_convert_fusion.1 = bf16[2048,704]{0,1:T(8,128)(2,1)} fusion(bf16[1024,704]{0,1:T(8,128)(2,1)S(1)} %get-tuple-element.55, bf16[1024,2048]{1,0:T(8,128)(2,1)} %constant_dynamic-update-slice_fusion.16), kind=kOutput, calls=%fused_computation.3 | convolution fusion | flops 2954231808 | bytes 8519680 | tf_op jit(solution)/shard_map/dot_general | solution.py:42
  290.1 9.0 %collective-permute-done.58 = bf16[64,2048]{1,0:T(8,128)(2,1)S(1)} collective-permute-done((bf16[64,2048]{1,0:T(8,128)(2,1)S(1)}, bf16[64,2048]{1,0:T(8,128)(2,1)S(1)}, u32[]{:S(2)}, u32[]{:S(2)}) %collective-permute-start.58) | collective-permute-done | bytes 262176 | tf_op jit(solution)/shard_map/ppermute | solution.py:61
  299.1 5.6 collective-permute-done.65
  321.6 5.6 collective-permute-done.66
  403.4 15.0 %attend_back.1 = (bf16[1,1024,256]{2,1,0:T(8,128)(2,1)}, bf16[1,1024,256]{2,1,0:T(8,128)(2,1)}, bf16[1,1024,256]{2,1,0:T(8,128)(2,1)}) custom-call(bf16[1,1024,256]{2,1,0:T(8,128)(2,1)} %get-tuple-element.25.q_in, bf16[1,1024,256]{2,1,0:T(8,128)(2,1)} %get-tuple-element.26.k_in, bf16[1,1024,256]{2,1,0:T(8,128)(2,1)} %get-tuple-element.27.v_in, ...), custom_call_target="tpu_custom_call" | custom-call | tf_op jit(solution)/shard_map/attend_back/pallas_call | solution.py:382
  451.9 8.5 %collective-permute-done.86 = bf16[64,2048]{1,0:T(8,128)(2,1)} collective-permute-done((bf16[64,2048]{1,0:T(8,128)(2,1)}, bf16[64,2048]{1,0:T(8,128)(2,1)}, u32[]{:S(2)}, u32[]{:S(2)}) %collective-permute-start.86) | collective-permute-done | bytes 262176 | tf_op jit(solution)/shard_map/ppermute | solution.py:61
  473.0 6.1 %collective-permute-done.87 = bf16[64,2048]{1,0:T(8,128)(2,1)} collective-permute-done((bf16[64,2048]{1,0:T(8,128)(2,1)}, bf16[64,2048]{1,0:T(8,128)(2,1)}, u32[]{:S(2)}, u32[]{:S(2)}) %collective-permute-start.87) | collective-permute-done | bytes 262176 | tf_op jit(solution)/shard_map/ppermute | solution.py:61
  488.4 6.5 %collective-permute-done.103 = bf16[512,1024]{1,0:T(8,128)(2,1)S(1)} collective-permute-done((bf16[512,1024]{1,0:T(8,128)(2,1)}, bf16[512,1024]{1,0:T(8,128)(2,1)S(1)}, u32[]{:S(2)}, u32[]{:S(2)}) %collective-permute-start.103) | collective-permute-done | bytes 1048608 | tf_op jit(solution)/shard_map/ppermute | solution.py:142
  509.0 7.0 %collective-permute-done.104 = bf16[256,1024]{1,0:T(8,128)(2,1)} collective-permute-done((bf16[256,1024]{1,0:T(8,128)(2,1)}, bf16[256,1024]{1,0:T(8,128)(2,1)}, u32[]{:S(2)}, u32[]{:S(2)}) %collective-permute-start.104) | collective-permute-done | bytes 524320 | tf_op jit(solution)/shard_map/ppermute | solution.py:142
  524.0 7.0 %collective-permute-done.107 = bf16[512,256]{1,0:T(8,128)(2,1)S(1)} collective-permute-done((bf16[512,256]{1,0:T(8,128)(2,1)S(1)}, bf16[512,256]{1,0:T(8,128)(2,1)S(1)}, u32[]{:S(2)}, u32[]{:S(2)}) %collective-permute-start.107) | collective-permute-done | bytes 262176 | tf_op jit(solution)/shard_map/ppermute | solution.py:232
  533.7 12.1 %collective-permute-done.99 = f32[1792]{0:T(1024)S(1)} collective-permute-done((f32[1792]{0:T(1024)S(1)}, f32[1792]{0:T(1024)S(1)}, u32[]{:S(2)}, u32[]{:S(2)}) %collective-permute-start.99) | collective-permute-done | bytes 7200 | tf_op jit(solution)/shard_map/ppermute | solution.py:142
  554.4 7.7 %collective-permute-done.109.refs_2_ = bf16[256,1024]{1,0:T(8,128)(2,1)S(1)} collective-permute-done((bf16[256,1024]{1,0:T(8,128)(2,1)S(1)}, bf16[256,1024]{1,0:T(8,128)(2,1)S(1)}, u32[]{:S(2)}, u32[]{:S(2)}) %collective-permute-start.109) | collective-permute-done | bytes 524320 | tf_op jit(solution)/shard_map/ppermute | solution.py:142
  563.3 7.6 %collective-permute-done.110.refs_3_ = bf16[256,1024]{1,0:T(8,128)(2,1)S(1)} collective-permute-done((bf16[256,1024]{1,0:T(8,128)(2,1)S(1)}, bf16[256,1024]{1,0:T(8,128)(2,1)S(1)}, u32[]{:S(2)}, u32[]{:S(2)}) %collective-permute-start.110) | collective-permute-done | bytes 524320 | tf_op jit(solution)/shard_map/ppermute | solution.py:142
  572.1 6.1 %assemble.1 = (f32[2048,768]{1,0:T(8,128)}, f32[256,2048]{1,0:T(8,128)}) custom-call(s32[8]{0:T(128)} %stack.63.starts, bf16[256,1024]{1,0:T(8,128)(2,1)} %copy-done.49, bf16[256,1024]{1,0:T(8,128)(2,1)} %copy-done.55, bf16[256,1024]{1,0:T(8,128)(2,1)} %copy-done.57, bf16[256,1024]{1,0:T(8,128)(2,1)} %copy-done.59, bf16[256,1024]{1,0:T(8,128)(2,1)} %copy-done.48, ...), custom_call_target="tpu_custom_call" | custom-call | tf_op jit(solution)/shard_map/assemble/pallas_call | solution.py:407
  (553 shorter events, 379.9 us)
Async XLA Ops:
  7.2 83.6 %all-gather.3.cloned.1.call-start = ((), (), s32[]{:S(2)}) async-start(), calls=%async_computation | async-start | bytes 4718592 | tf_op jit(solution)/shard_map/all_gather | solution.py:460
  13.6 157.5 %all-gather.5.cloned.1.call-start = ((), (), s32[]{:S(2)}) async-start(), calls=%async_computation.1 | async-start | bytes 4718592 | tf_op jit(solution)/shard_map/all_gather | solution.py:472
  15.9 29.8 %collective-permute-start.2 = (bf16[528,256]{1,0:T(8,128)(2,1)}, bf16[528,256]{1,0:T(8,128)(2,1)}, u32[]{:S(2)}, u32[]{:S(2)}) collective-permute-start(bf16[528,256]{1,0:T(8,128)(2,1)} %get-tuple-element.139), channel_id=1, source_target_pairs={{0,2},{1,5},{2,0},{3,3},{4,6},{5,1},{6,4},{7,7},{8,10},{9,13},{10,... | collective-permute-start | bytes 811016 | tf_op jit(solution)/shard_map/ppermute | solution.py:213
  20.9 24.9 %collective-permute-start.1 = (bf16[528,256]{1,0:T(8,128)(2,1)}, bf16[528,256]{1,0:T(8,128)(2,1)}, u32[]{:S(2)}, u32[]{:S(2)}) collective-permute-start(bf16[528,256]{1,0:T(8,128)(2,1)} %get-tuple-element.140), channel_id=1, source_target_pairs={{0,1},{1,4},{2,7},{3,2},{4,5},{5,0},{6,3},{7,6},{8,9},{9,12},{10,1... | collective-permute-start | bytes 811016 | tf_op jit(solution)/shard_map/ppermute | solution.py:213
  21.5 24.3 %collective-permute-start = (bf16[528,256]{1,0:T(8,128)(2,1)}, bf16[528,256]{1,0:T(8,128)(2,1)}, u32[]{:S(2)}, u32[]{:S(2)}) collective-permute-start(bf16[528,256]{1,0:T(8,128)(2,1)} %get-tuple-element.138), channel_id=1, source_target_pairs={{0,0},{1,3},{2,6},{3,1},{4,4},{5,7},{6,2},{7,5},{8,8},{9,11},{10,1... | collective-permute-start | bytes 811016 | tf_op jit(solution)/shard_map/ppermute | solution.py:213
  29.2 549.1 %all-reduce.3.cloned.1.call-start = ((), (), s32[]{:S(2)}) async-start(), calls=%async_computation.2 | async-start | bytes 17301504 | tf_op jit(solution)/shard_map/psum | solution.py:494
  29.6 23.8 %collective-permute-start.10 = (s32[256]{0:T(256)S(1)}, s32[256]{0:T(256)S(1)}, u32[]{:S(2)}, u32[]{:S(2)}) collective-permute-start(s32[256]{0:T(256)S(1)} %add_select_fusion.2), channel_id=1, source_target_pairs={{0,2},{1,3},{2,0},{3,1},{4,6},{5,7},{6,4},{7,5},{8,10},{9,11},{10,... | collective-permute-start | bytes 3080 | tf_op jit(solution)/shard_map/ppermute | solution.py:78
  58.3 23.9 %collective-permute-start.4 = (bf16[256,768]{1,0:T(8,128)(2,1)}, bf16[256,768]{1,0:T(8,128)(2,1)S(1)}, u32[]{:S(2)}, u32[]{:S(2)}) collective-permute-start(bf16[256,768]{1,0:T(8,128)(2,1)} %get-tuple-element.146), channel_id=1, source_target_pairs={{0,8},{8,0},{16,24},{24,16},{1,9},{9,1},{17,25},{25,17},{2,10},{10... | collective-permute-start | bytes 1179656 | tf_op jit(solution)/shard_map/ppermute | solution.py:142
  59.8 19.1 %collective-permute-start.6 = (bf16[256,768]{1,0:T(8,128)(2,1)S(1)}, bf16[256,768]{1,0:T(8,128)(2,1)S(1)}, u32[]{:S(2)}, u32[]{:S(2)}) collective-permute-start(bf16[256,768]{1,0:T(8,128)(2,1)S(1)} %get-tuple-element.144), channel_id=1, source_target_pairs={{0,8},{8,0},{16,24},{24,16},{1,9},{9,1},{17,25},{25,17},{2,10},{10... | collective-permute-start | bytes 1179656 | tf_op jit(solution)/shard_map/ppermute | solution.py:142
  63.4 25.8 %collective-permute-start.7 = (bf16[256,768]{1,0:T(8,128)(2,1)S(1)}, bf16[256,768]{1,0:T(8,128)(2,1)S(1)}, u32[]{:S(2)}, u32[]{:S(2)}) collective-permute-start(bf16[256,768]{1,0:T(8,128)(2,1)S(1)} %get-tuple-element.144), channel_id=1, source_target_pairs={{0,16},{8,24},{16,0},{24,8},{1,17},{9,25},{17,1},{25,9},{2,18},{10... | collective-permute-start | bytes 1179656 | tf_op jit(solution)/shard_map/ppermute | solution.py:142
  64.8 22.1 %collective-permute-start.5 = (bf16[256,768]{1,0:T(8,128)(2,1)}, bf16[256,768]{1,0:T(8,128)(2,1)S(1)}, u32[]{:S(2)}, u32[]{:S(2)}) collective-permute-start(bf16[256,768]{1,0:T(8,128)(2,1)} %collective-permute-done.3), channel_id=1, source_target_pairs={{0,8},{8,0},{16,24},{24,16},{1,9},{9,1},{17,25},{25,17},{2,10},{10... | collective-permute-start | bytes 1179656 | tf_op jit(solution)/shard_map/ppermute | solution.py:142
  266.0 22.1 %collective-permute-start.43 = (bf16[64,2048]{1,0:T(8,128)(2,1)}, bf16[64,2048]{1,0:T(8,128)(2,1)}, u32[]{:S(2)}, u32[]{:S(2)}) collective-permute-start(bf16[64,2048]{1,0:T(8,128)(2,1)} %get-tuple-element.109), channel_id=1, source_target_pairs={{0,1},{1,0},{2,3},{3,2},{4,5},{5,4},{6,7},{7,6},{8,9},{9,8},{10,11... | collective-permute-start | bytes 786440 | tf_op jit(solution)/shard_map/ppermute | solution.py:55
  266.5 21.7 %collective-permute-start.50 = (bf16[64,2048]{1,0:T(8,128)(2,1)}, bf16[64,2048]{1,0:T(8,128)(2,1)}, u32[]{:S(2)}, u32[]{:S(2)}) collective-permute-start(bf16[64,2048]{1,0:T(8,128)(2,1)} %get-tuple-element.110), channel_id=1, source_target_pairs={{0,1},{1,0},{2,3},{3,2},{4,5},{5,4},{6,7},{7,6},{8,9},{9,8},{10,11... | collective-permute-start | bytes 786440 | tf_op jit(solution)/shard_map/ppermute | solution.py:55
  268.9 36.1 %collective-permute-start.42 = (bf16[64,2048]{1,0:T(8,128)(2,1)}, bf16[64,2048]{1,0:T(8,128)(2,1)}, u32[]{:S(2)}, u32[]{:S(2)}) collective-permute-start(bf16[64,2048]{1,0:T(8,128)(2,1)} %get-tuple-element.105), channel_id=1, source_target_pairs={{0,1},{1,0},{2,3},{3,2},{4,5},{5,4},{6,7},{7,6},{8,9},{9,8},{10,11... | collective-permute-start | bytes 786440 | tf_op jit(solution)/shard_map/ppermute | solution.py:55
  289.8 37.6 %collective-permute-start.41 = (bf16[64,2048]{1,0:T(8,128)(2,1)S(1)}, bf16[64,2048]{1,0:T(8,128)(2,1)S(1)}, u32[]{:S(2)}, u32[]{:S(2)}) collective-permute-start(bf16[64,2048]{1,0:T(8,128)(2,1)S(1)} %copy-done.62), channel_id=1, source_target_pairs={{0,1},{1,0},{2,3},{3,2},{4,5},{5,4},{6,7},{7,6},{8,9},{9,8},{10,11... | collective-permute-start | bytes 786440 | tf_op jit(solution)/shard_map/ppermute | solution.py:55
  317.3 37.2 %collective-permute-start.40 = (bf16[64,2048]{1,0:T(8,128)(2,1)}, bf16[64,2048]{1,0:T(8,128)(2,1)}, u32[]{:S(2)}, u32[]{:S(2)}) collective-permute-start(bf16[64,2048]{1,0:T(8,128)(2,1)} %get-tuple-element.97), channel_id=1, source_target_pairs={{0,1},{1,0},{2,3},{3,2},{4,5},{5,4},{6,7},{7,6},{8,9},{9,8},{10,11... | collective-permute-start | bytes 786440 | tf_op jit(solution)/shard_map/ppermute | solution.py:55
  354.6 19.4 %collective-permute-start.69 = (bf16[64,2048]{1,0:T(8,128)(2,1)}, bf16[64,2048]{1,0:T(8,128)(2,1)S(1)}, u32[]{:S(2)}, u32[]{:S(2)}) collective-permute-start(bf16[64,2048]{1,0:T(8,128)(2,1)} %get-tuple-element.147), channel_id=1, source_target_pairs={{0,1},{1,0},{2,3},{3,2},{4,5},{5,4},{6,7},{7,6},{8,9},{9,8},{10,11... | collective-permute-start | bytes 786440 | tf_op jit(solution)/shard_map/ppermute | solution.py:55
  437.2 32.9 %collective-permute-start.83 = (bf16[64,2048]{1,0:T(8,128)(2,1)}, bf16[64,2048]{1,0:T(8,128)(2,1)S(1)}, u32[]{:S(2)}, u32[]{:S(2)}) collective-permute-start(bf16[64,2048]{1,0:T(8,128)(2,1)} %get-tuple-element.69), channel_id=1, source_target_pairs={{0,1},{1,0},{2,3},{3,2},{4,5},{5,4},{6,7},{7,6},{8,9},{9,8},{10,11... | collective-permute-start | bytes 786440 | tf_op jit(solution)/shard_map/ppermute | solution.py:55
  450.2 22.7 %collective-permute-start.90 = (bf16[64,2048]{1,0:T(8,128)(2,1)}, bf16[64,2048]{1,0:T(8,128)(2,1)}, u32[]{:S(2)}, u32[]{:S(2)}) collective-permute-start(bf16[64,2048]{1,0:T(8,128)(2,1)} %get-tuple-element.70), channel_id=1, source_target_pairs={{0,1},{1,0},{2,3},{3,2},{4,5},{5,4},{6,7},{7,6},{8,9},{9,8},{10,11... | collective-permute-start | bytes 786440 | tf_op jit(solution)/shard_map/ppermute | solution.py:55
  450.5 34.4 %collective-permute-start.101 = (bf16[512,1024]{1,0:T(8,128)(2,1)}, bf16[512,1024]{1,0:T(8,128)(2,1)}, u32[]{:S(2)}, u32[]{:S(2)}) collective-permute-start(bf16[512,1024]{1,0:T(8,128)(2,1)} %constant_dynamic-slice_fusion.2), channel_id=1, source_target_pairs={{0,8},{8,0},{16,24},{24,16},{1,9},{9,1},{17,25},{25,17},{2,10},{10... | collective-permute-start | bytes 3145736 | tf_op jit(solution)/shard_map/ppermute | solution.py:142
  470.1 24.8 %collective-permute-start.103 = (bf16[512,1024]{1,0:T(8,128)(2,1)}, bf16[512,1024]{1,0:T(8,128)(2,1)S(1)}, u32[]{:S(2)}, u32[]{:S(2)}) collective-permute-start(bf16[512,1024]{1,0:T(8,128)(2,1)} %fusion.17), channel_id=1, source_target_pairs={{0,16},{8,24},{16,0},{24,8},{1,17},{9,25},{17,1},{25,9},{2,18},{10... | collective-permute-start | bytes 3145736 | tf_op jit(solution)/shard_map/ppermute | solution.py:142
  473.0 24.8 %collective-permute-start.82 = (bf16[64,2048]{1,0:T(8,128)(2,1)S(1)}, bf16[64,2048]{1,0:T(8,128)(2,1)S(1)}, u32[]{:S(2)}, u32[]{:S(2)}) collective-permute-start(bf16[64,2048]{1,0:T(8,128)(2,1)S(1)} %get-tuple-element.65), channel_id=1, source_target_pairs={{0,1},{1,0},{2,3},{3,2},{4,5},{5,4},{6,7},{7,6},{8,9},{9,8},{10,11... | collective-permute-start | bytes 786440 | tf_op jit(solution)/shard_map/ppermute | solution.py:55
  549.1 21.9 %collective-permute-start.110 = (bf16[256,1024]{1,0:T(8,128)(2,1)S(1)}, bf16[256,1024]{1,0:T(8,128)(2,1)S(1)}, u32[]{:S(2)}, u32[]{:S(2)}) collective-permute-start(bf16[256,1024]{1,0:T(8,128)(2,1)S(1)} %collective-permute-done.108.refs_1_), channel_id=1, source_target_pairs={{0,8},{8,0},{16,24},{24,16},{1,9},{9,1},{17,25},{25,17},{2,10},{10... | collective-permute-start | bytes 1572872 | tf_op jit(solution)/shard_map/ppermute | solution.py:142
  549.8 22.3 %collective-permute-start.113 = (bf16[256,1024]{1,0:T(8,128)(2,1)S(1)}, bf16[256,1024]{1,0:T(8,128)(2,1)}, u32[]{:S(2)}, u32[]{:S(2)}) collective-permute-start(bf16[256,1024]{1,0:T(8,128)(2,1)S(1)} %collective-permute-done.111.refs_5_), channel_id=1, source_target_pairs={{0,16},{8,24},{16,0},{24,8},{1,17},{9,25},{17,1},{25,9},{2,18},{10... | collective-permute-start | bytes 1572872 | tf_op jit(solution)/shard_map/ppermute | solution.py:142
  (164 other events, 2201.9 us)
Sparse Core Ops, SparseCore 0:
  13.7 55.8 all-gather.2
  71.8 49.5 all-gather.4
  263.9 173.8 all-reduce.2

commit v2 on v1

--- a/solution.py
+++ b/solution.py
@@ -64,10 +64,6 @@
 def cut(value):
     rows = value.shape[0] // SPLITS
     return [value[k * rows : (k + 1) * rows] for k in range(SPLITS)]
-
-
-def after(value, *earlier):
-    return lax.optimization_barrier((value,) + earlier)[0]
 
 
 def gather_places(local):
@@ -108,7 +104,7 @@
     return full
 
 
-def scatter_tokens(block_of, count, meanwhile=None):
+def scatter_tokens(block_of, count):
     size = lax.axis_size("seq")
     me = lax.axis_index("seq")
     chips = size // CORES
@@ -117,8 +113,6 @@
     carried = [None] * SPLITS
     for step in range(1, chips + 1):
         row = ((chip - step) % chips) * CORES * count
-        if meanwhile is not None and step == 2:
-            row = after(row, *meanwhile)
         block = block_of(row)
         totals = []
         for k in range(SPLITS):
@@ -489,7 +483,6 @@
         lambda row: mm(rows_of(grad_gate, row, CORES * count), w_gate, ROWS_COLS)
         + mm(rows_of(grad_upward, row, CORES * count), w_up, ROWS_COLS),
         count,
-        feed_grads,
     )
     feed_grads = lax.psum(feed_grads, "row")
     grad_middle = grad_top + norm_back(grad_second * gain_two, normed_two, inverse_two)

time: 607 us -> 595 us (0.980)
  matrix products: 99.7 us -> 86.7 us
  starting transfers between devices: 56.9 us -> 66.6 us
    dot_general x30, matrix products: 99.7 us -> 86.7 us  [mm(): lax.dot_general(left, right, (dims, ((), ())), preferred_element_type=F32)]
    ppermute x36, starting transfers between devices: 3.82 us -> 16.7 us  [ring(): return [lax.ppermute(part, 'seq', to) for part in value]]
  transfers between devices with their start and end apart: 117 -> 117, of which waited for: 49 -> 49; matrix products, arithmetic and copies ran while one was open for 26% -> 27% of each run, Pallas kernels for 6% -> 6%
where the time goes in v2:
time: 595 us; the launch traced here: 585 us
  waiting for transfers between devices  253 us (43%)
  matrix products  86.7 us (15%)
  local copies, waits for them, and re-layouts  72.9 us (12%)
  starting transfers between devices  66.6 us (11%)
  other arithmetic  56.6 us (10%)
  Pallas kernels  32.6 us (5%)
  between operations  17.1 us (3%)
    ppermute x36, waiting for transfers between devices, ring(): return [lax.ppermute(part, 'seq', to) for part in value]  168 us
    dot_general x30, matrix products, mm(): lax.dot_general(left, right, (dims, ((), ())), preferred_element_type=F32)  86.7 us
    ppermute x18, waiting for transfers between devices, row_swap(): return lax.ppermute(value, 'row', [(d, d ^ bit) for d in range(size)])  59 us
    ppermute x18, starting transfers between devices, row_swap(): return lax.ppermute(value, 'row', [(d, d ^ bit) for d in range(size)])  20.4 us
    ppermute x36, starting transfers between devices, ring(): return [lax.ppermute(part, 'seq', to) for part in value]  16.7 us
    pallas_call x1, Pallas kernels, attend_back(): pl.pallas_call(attend_back_kernel, grid=(width // LANES,), in_specs=[spec...  14.7 us
    ppermute x3, waiting for transfers between devices, to_heads(): lax.ppermute(units[..., i * unit:(i + 1) * unit], 'seq', [(d, (3 * d + i)...  14.4 us
    dynamic_update_slice x16, local copies, waits for them, and re-layouts, gather_tokens(): lax.dynamic_update_slice_in_dim(full, other, (base + 1 - core) * count +...  13.4 us
  transfers between devices with their start and end apart: 117, of which 49 were waited for; matrix products, arithmetic and copies ran while one was open for 27% of the time, Pallas kernels for 6%

profile of v2, /device:TPU:0, one launch (start us, length us, event | category | flops | bytes accessed | tf_op | source)
XLA Modules:
  0.0 585.5 jit_solution(5458429247502827436)
XLA Ops:
  31.4 14.4 %collective-permute-done.2 = bf16[528,256]{1,0:T(8,128)(2,1)} collective-permute-done((bf16[528,256]{1,0:T(8,128)(2,1)}, bf16[528,256]{1,0:T(8,128)(2,1)}, u32[]{:S(2)}, u32[]{:S(2)}) %collective-permute-start.2) | collective-permute-done | bytes 270368 | tf_op jit(solution)/shard_map/ppermute | solution.py:207
  67.8 11.2 %collective-permute-done.6 = bf16[256,768]{1,0:T(8,128)(2,1)S(1)} collective-permute-done((bf16[256,768]{1,0:T(8,128)(2,1)S(1)}, bf16[256,768]{1,0:T(8,128)(2,1)S(1)}, u32[]{:S(2)}, u32[]{:S(2)}) %collective-permute-start.6) | collective-permute-done | bytes 393248 | tf_op jit(solution)/shard_map/ppermute | solution.py:136
  90.8 6.1 %fusion.123 = f32[1024,768]{1,0:T(8,128)S(1)} fusion(bf16[1024,2048]{1,0:T(8,128)(2,1)} %all-gather.3.cloned.1.call-done, bf16[2048,768]{1,0:T(8,128)(2,1)} %constant_dynamic-update-slice_fusion.32), kind=kOutput, calls=%fused_computation.331 | convolution fusion | flops 3221225472 | bytes 10485760 | tf_op jit(solution)/shard_map/dot_general | solution.py:42
  98.7 11.8 %attend.1 = (bf16[1,1024,256]{2,1,0:T(8,128)(2,1)}, bf16[1,1024,256]{2,1,0:T(8,128)(2,1)}, bf16[1,1024,256]{2,1,0:T(8,128)(2,1)}, bf16[1,1024,256]{2,1,0:T(8,128)(2,1)}, f32[1,1024,256]{2,1,0:T(8,128)}) custom-call(f32[1,1024,256]{2,1,0:T(8,128)} %get-tuple-element.58.q_in, f32[1,1024,256]{2,1,0:T(8,128)} %get-tuple-element.57.k_in, ...), custom_call_target="tpu_custom_call" | custom-call | tf_op jit(solution)/shard_map/attend/pallas_call | solution.py:359
  116.9 12.6 %collective-permute-start.23 = (bf16[64,2048]{1,0:T(8,128)(2,1)S(1)}, bf16[64,2048]{1,0:T(8,128)(2,1)S(1)}, u32[]{:S(2)}, u32[]{:S(2)}) collective-permute-start(bf16[64,2048]{1,0:T(8,128)(2,1)S(1)} %get-tuple-element.122), channel_id=1, source_target_pairs={{0,2},{1,3},{2,4},{3,5},{4,6},{5,7},{6,0},{7,1},{8,10},{9,11},{10,... | collective-permute-start | bytes 786440 | tf_op jit(solution)/shard_map/ppermute | solution.py:61
  130.6 8.4 %collective-permute-done.23 = bf16[64,2048]{1,0:T(8,128)(2,1)S(1)} collective-permute-done((bf16[64,2048]{1,0:T(8,128)(2,1)S(1)}, bf16[64,2048]{1,0:T(8,128)(2,1)S(1)}, u32[]{:S(2)}, u32[]{:S(2)}) %collective-permute-start.23) | collective-permute-done | bytes 262176 | tf_op jit(solution)/shard_map/ppermute | solution.py:61
  142.4 7.8 %collective-permute-done.17 = bf16[64,2048]{1,0:T(8,128)(2,1)S(1)} collective-permute-done((bf16[64,2048]{1,0:T(8,128)(2,1)S(1)}, bf16[64,2048]{1,0:T(8,128)(2,1)S(1)}, u32[]{:S(2)}, u32[]{:S(2)}) %collective-permute-start.17) | collective-permute-done | bytes 262176 | tf_op jit(solution)/shard_map/ppermute | solution.py:61
  155.9 10.2 %collective-permute-done.18 = bf16[64,2048]{1,0:T(8,128)(2,1)} collective-permute-done((bf16[64,2048]{1,0:T(8,128)(2,1)}, bf16[64,2048]{1,0:T(8,128)(2,1)}, u32[]{:S(2)}, u32[]{:S(2)}) %collective-permute-start.18) | collective-permute-done | bytes 262176 | tf_op jit(solution)/shard_map/ppermute | solution.py:61
  176.4 5.9 %fusion.125 = f32[1024,704]{0,1:T(8,128)S(1)} fusion(bf16[1024,2048]{1,0:T(8,128)(2,1)} %all-gather.5.cloned.1.call-done, bf16[704,2048]{1,0:T(8,128)(2,1)} %param.26), kind=kOutput, calls=%fused_computation.333 | convolution fusion | flops 2952790016 | bytes 9961472 | tf_op jit(solution)/shard_map/dot_general | solution.py:42
  225.3 6.8 %multiply_convert_fusion = (bf16[1024,704]{0,1:T(8,128)(2,1)S(1)}, bf16[1024,704]{0,1:T(8,128)(2,1)S(1)}, bf16[1024,704]{0,1:T(8,128)(2,1)S(1)}) fusion(f32[1024,704]{0,1:T(8,128)S(1)} %fusion.125, f32[1024,704]{0,1:T(8,128)S(1)} %fusion.124, bf16[1024,2048]{1,0:T(8,128)(2,1)} %constant_dynamic-update-slice_fusion.16, bf16[2048,704]{0,1:T(8,128)(2,1)S(1)} %copy-done), kind=kOutput, calls=%fused_computation.7 | convolution fusion | flops 2963603456 | bytes 17170432 | tf_op jit(solution)/shard_map/dot_general | solution.py:42
  240.3 7.0 %convolution_convert_fusion.2 = bf16[2048,704]{0,1:T(8,128)(2,1)} fusion(bf16[1024,704]{0,1:T(8,128)(2,1)S(1)} %get-tuple-element.54, bf16[1024,2048]{1,0:T(8,128)(2,1)} %constant_dynamic-update-slice_fusion.16), kind=kOutput, calls=%fused_computation.4 | convolution fusion | flops 2954231808 | bytes 8519680 | tf_op jit(solution)/shard_map/dot_general | solution.py:42
  251.0 6.6 %convolution_convert_fusion.1 = bf16[2048,704]{0,1:T(8,128)(2,1)} fusion(bf16[1024,704]{0,1:T(8,128)(2,1)S(1)} %get-tuple-element.53, bf16[1024,2048]{1,0:T(8,128)(2,1)} %constant_dynamic-update-slice_fusion.16), kind=kOutput, calls=%fused_computation.3 | convolution fusion | flops 2954231808 | bytes 8519680 | tf_op jit(solution)/shard_map/dot_general | solution.py:42
  279.8 8.7 %collective-permute-done.58 = bf16[64,2048]{1,0:T(8,128)(2,1)S(1)} collective-permute-done((bf16[64,2048]{1,0:T(8,128)(2,1)S(1)}, bf16[64,2048]{1,0:T(8,128)(2,1)S(1)}, u32[]{:S(2)}, u32[]{:S(2)}) %collective-permute-start.58) | collective-permute-done | bytes 262176 | tf_op jit(solution)/shard_map/ppermute | solution.py:61
  299.8 5.6 collective-permute-done.51
  393.1 14.7 %attend_back.1 = (bf16[1,1024,256]{2,1,0:T(8,128)(2,1)}, bf16[1,1024,256]{2,1,0:T(8,128)(2,1)}, bf16[1,1024,256]{2,1,0:T(8,128)(2,1)}) custom-call(bf16[1,1024,256]{2,1,0:T(8,128)(2,1)} %get-tuple-element.23.q_in, bf16[1,1024,256]{2,1,0:T(8,128)(2,1)} %get-tuple-element.24.k_in, bf16[1,1024,256]{2,1,0:T(8,128)(2,1)} %get-tuple-element.25.v_in, ...), custom_call_target="tpu_custom_call" | custom-call | tf_op jit(solution)/shard_map/attend_back/pallas_call | solution.py:376
  441.7 8.6 %collective-permute-done.86 = bf16[64,2048]{1,0:T(8,128)(2,1)} collective-permute-done((bf16[64,2048]{1,0:T(8,128)(2,1)}, bf16[64,2048]{1,0:T(8,128)(2,1)}, u32[]{:S(2)}, u32[]{:S(2)}) %collective-permute-start.86) | collective-permute-done | bytes 262176 | tf_op jit(solution)/shard_map/ppermute | solution.py:61
  461.7 7.3 %collective-permute-done.87 = bf16[64,2048]{1,0:T(8,128)(2,1)} collective-permute-done((bf16[64,2048]{1,0:T(8,128)(2,1)}, bf16[64,2048]{1,0:T(8,128)(2,1)}, u32[]{:S(2)}, u32[]{:S(2)}) %collective-permute-start.87) | collective-permute-done | bytes 262176 | tf_op jit(solution)/shard_map/ppermute | solution.py:61
  478.2 6.6 %collective-permute-done.103 = bf16[512,1024]{1,0:T(8,128)(2,1)S(1)} collective-permute-done((bf16[512,1024]{1,0:T(8,128)(2,1)}, bf16[512,1024]{1,0:T(8,128)(2,1)S(1)}, u32[]{:S(2)}, u32[]{:S(2)}) %collective-permute-start.103) | collective-permute-done | bytes 1048608 | tf_op jit(solution)/shard_map/ppermute | solution.py:136
  498.9 5.9 %collective-permute-done.104 = bf16[256,1024]{1,0:T(8,128)(2,1)} collective-permute-done((bf16[256,1024]{1,0:T(8,128)(2,1)}, bf16[256,1024]{1,0:T(8,128)(2,1)}, u32[]{:S(2)}, u32[]{:S(2)}) %collective-permute-start.104) | collective-permute-done | bytes 524320 | tf_op jit(solution)/shard_map/ppermute | solution.py:136
  513.7 5.9 %collective-permute-done.107 = bf16[512,256]{1,0:T(8,128)(2,1)S(1)} collective-permute-done((bf16[512,256]{1,0:T(8,128)(2,1)S(1)}, bf16[512,256]{1,0:T(8,128)(2,1)S(1)}, u32[]{:S(2)}, u32[]{:S(2)}) %collective-permute-start.107) | collective-permute-done | bytes 262176 | tf_op jit(solution)/shard_map/ppermute | solution.py:226
  523.5 11.7 %collective-permute-done.99 = f32[1792]{0:T(1024)S(1)} collective-permute-done((f32[1792]{0:T(1024)S(1)}, f32[1792]{0:T(1024)S(1)}, u32[]{:S(2)}, u32[]{:S(2)}) %collective-permute-start.99) | collective-permute-done | bytes 7200 | tf_op jit(solution)/shard_map/ppermute | solution.py:136
  543.0 7.7 %collective-permute-done.109.refs_2_ = bf16[256,1024]{1,0:T(8,128)(2,1)S(1)} collective-permute-done((bf16[256,1024]{1,0:T(8,128)(2,1)S(1)}, bf16[256,1024]{1,0:T(8,128)(2,1)S(1)}, u32[]{:S(2)}, u32[]{:S(2)}) %collective-permute-start.109) | collective-permute-done | bytes 524320 | tf_op jit(solution)/shard_map/ppermute | solution.py:136
  551.7 8.1 %collective-permute-done.110.refs_3_ = bf16[256,1024]{1,0:T(8,128)(2,1)S(1)} collective-permute-done((bf16[256,1024]{1,0:T(8,128)(2,1)S(1)}, bf16[256,1024]{1,0:T(8,128)(2,1)S(1)}, u32[]{:S(2)}, u32[]{:S(2)}) %collective-permute-start.110) | collective-permute-done | bytes 524320 | tf_op jit(solution)/shard_map/ppermute | solution.py:136
  560.7 6.1 %assemble.1 = (f32[2048,768]{1,0:T(8,128)}, f32[256,2048]{1,0:T(8,128)}) custom-call(s32[8]{0:T(128)} %stack.63.starts, bf16[256,1024]{1,0:T(8,128)(2,1)} %copy-done.54, bf16[256,1024]{1,0:T(8,128)(2,1)} %copy-done.57, bf16[256,1024]{1,0:T(8,128)(2,1)} %copy-done.59, bf16[256,1024]{1,0:T(8,128)(2,1)} %copy-done.61, bf16[256,1024]{1,0:T(8,128)(2,1)} %copy-done.53, ...), custom_call_target="tpu_custom_call" | custom-call | tf_op jit(solution)/shard_map/assemble/pallas_call | solution.py:401
  (555 shorter events, 362.7 us)
Async XLA Ops:
  7.2 83.6 %all-gather.3.cloned.1.call-start = ((), (), s32[]{:S(2)}) async-start(), calls=%async_computation | async-start | bytes 4718592 | tf_op jit(solution)/shard_map/all_gather | solution.py:454
  13.6 162.8 %all-gather.5.cloned.1.call-start = ((), (), s32[]{:S(2)}) async-start(), calls=%async_computation.1 | async-start | bytes 4718592 | tf_op jit(solution)/shard_map/all_gather | solution.py:466
  15.9 29.8 %collective-permute-start.2 = (bf16[528,256]{1,0:T(8,128)(2,1)}, bf16[528,256]{1,0:T(8,128)(2,1)}, u32[]{:S(2)}, u32[]{:S(2)}) collective-permute-start(bf16[528,256]{1,0:T(8,128)(2,1)} %get-tuple-element.137), channel_id=1, source_target_pairs={{0,2},{1,5},{2,0},{3,3},{4,6},{5,1},{6,4},{7,7},{8,10},{9,13},{10,... | collective-permute-start | bytes 811016 | tf_op jit(solution)/shard_map/ppermute | solution.py:207
  20.9 24.9 %collective-permute-start.1 = (bf16[528,256]{1,0:T(8,128)(2,1)}, bf16[528,256]{1,0:T(8,128)(2,1)}, u32[]{:S(2)}, u32[]{:S(2)}) collective-permute-start(bf16[528,256]{1,0:T(8,128)(2,1)} %get-tuple-element.138), channel_id=1, source_target_pairs={{0,1},{1,4},{2,7},{3,2},{4,5},{5,0},{6,3},{7,6},{8,9},{9,12},{10,1... | collective-permute-start | bytes 811016 | tf_op jit(solution)/shard_map/ppermute | solution.py:207
  21.5 24.3 %collective-permute-start = (bf16[528,256]{1,0:T(8,128)(2,1)}, bf16[528,256]{1,0:T(8,128)(2,1)}, u32[]{:S(2)}, u32[]{:S(2)}) collective-permute-start(bf16[528,256]{1,0:T(8,128)(2,1)} %get-tuple-element.136), channel_id=1, source_target_pairs={{0,0},{1,3},{2,6},{3,1},{4,4},{5,7},{6,2},{7,5},{8,8},{9,11},{10,1... | collective-permute-start | bytes 811016 | tf_op jit(solution)/shard_map/ppermute | solution.py:207
  29.2 537.6 %all-reduce.3.cloned.1.call-start = ((), (), s32[]{:S(2)}) async-start(), calls=%async_computation.2 | async-start | bytes 17301504 | tf_op jit(solution)/shard_map/psum | solution.py:487
  29.6 23.8 %collective-permute-start.10 = (s32[256]{0:T(256)S(1)}, s32[256]{0:T(256)S(1)}, u32[]{:S(2)}, u32[]{:S(2)}) collective-permute-start(s32[256]{0:T(256)S(1)} %add_select_fusion.2), channel_id=1, source_target_pairs={{0,2},{1,3},{2,0},{3,1},{4,6},{5,7},{6,4},{7,5},{8,10},{9,11},{10,... | collective-permute-start | bytes 3080 | tf_op jit(solution)/shard_map/ppermute | solution.py:74
  58.3 23.9 %collective-permute-start.4 = (bf16[256,768]{1,0:T(8,128)(2,1)}, bf16[256,768]{1,0:T(8,128)(2,1)S(1)}, u32[]{:S(2)}, u32[]{:S(2)}) collective-permute-start(bf16[256,768]{1,0:T(8,128)(2,1)} %get-tuple-element.144), channel_id=1, source_target_pairs={{0,8},{8,0},{16,24},{24,16},{1,9},{9,1},{17,25},{25,17},{2,10},{10... | collective-permute-start | bytes 1179656 | tf_op jit(solution)/shard_map/ppermute | solution.py:136
  63.4 25.8 %collective-permute-start.7 = (bf16[256,768]{1,0:T(8,128)(2,1)S(1)}, bf16[256,768]{1,0:T(8,128)(2,1)S(1)}, u32[]{:S(2)}, u32[]{:S(2)}) collective-permute-start(bf16[256,768]{1,0:T(8,128)(2,1)S(1)} %get-tuple-element.142), channel_id=1, source_target_pairs={{0,16},{8,24},{16,0},{24,8},{1,17},{9,25},{17,1},{25,9},{2,18},{10... | collective-permute-start | bytes 1179656 | tf_op jit(solution)/shard_map/ppermute | solution.py:136
  64.8 22.1 %collective-permute-start.5 = (bf16[256,768]{1,0:T(8,128)(2,1)}, bf16[256,768]{1,0:T(8,128)(2,1)S(1)}, u32[]{:S(2)}, u32[]{:S(2)}) collective-permute-start(bf16[256,768]{1,0:T(8,128)(2,1)} %collective-permute-done.3), channel_id=1, source_target_pairs={{0,8},{8,0},{16,24},{24,16},{1,9},{9,1},{17,25},{25,17},{2,10},{10... | collective-permute-start | bytes 1179656 | tf_op jit(solution)/shard_map/ppermute | solution.py:136
  116.9 22.1 %collective-permute-start.23 = (bf16[64,2048]{1,0:T(8,128)(2,1)S(1)}, bf16[64,2048]{1,0:T(8,128)(2,1)S(1)}, u32[]{:S(2)}, u32[]{:S(2)}) collective-permute-start(bf16[64,2048]{1,0:T(8,128)(2,1)S(1)} %get-tuple-element.122), channel_id=1, source_target_pairs={{0,2},{1,3},{2,4},{3,5},{4,6},{5,7},{6,0},{7,1},{8,10},{9,11},{10,... | collective-permute-start | bytes 786440 | tf_op jit(solution)/shard_map/ppermute | solution.py:61
  248.2 29.2 %collective-permute-start.43 = (bf16[64,2048]{1,0:T(8,128)(2,1)}, bf16[64,2048]{1,0:T(8,128)(2,1)}, u32[]{:S(2)}, u32[]{:S(2)}) collective-permute-start(bf16[64,2048]{1,0:T(8,128)(2,1)} %get-tuple-element.107), channel_id=1, source_target_pairs={{0,1},{1,0},{2,3},{3,2},{4,5},{5,4},{6,7},{7,6},{8,9},{9,8},{10,11... | collective-permute-start | bytes 786440 | tf_op jit(solution)/shard_map/ppermute | solution.py:55
  248.7 28.8 %collective-permute-start.50 = (bf16[64,2048]{1,0:T(8,128)(2,1)}, bf16[64,2048]{1,0:T(8,128)(2,1)}, u32[]{:S(2)}, u32[]{:S(2)}) collective-permute-start(bf16[64,2048]{1,0:T(8,128)(2,1)} %get-tuple-element.108), channel_id=1, source_target_pairs={{0,1},{1,0},{2,3},{3,2},{4,5},{5,4},{6,7},{7,6},{8,9},{9,8},{10,11... | collective-permute-start | bytes 786440 | tf_op jit(solution)/shard_map/ppermute | solution.py:55
  249.6 44.7 %collective-permute-start.42 = (bf16[64,2048]{1,0:T(8,128)(2,1)}, bf16[64,2048]{1,0:T(8,128)(2,1)}, u32[]{:S(2)}, u32[]{:S(2)}) collective-permute-start(bf16[64,2048]{1,0:T(8,128)(2,1)} %get-tuple-element.103), channel_id=1, source_target_pairs={{0,1},{1,0},{2,3},{3,2},{4,5},{5,4},{6,7},{7,6},{8,9},{9,8},{10,11... | collective-permute-start | bytes 786440 | tf_op jit(solution)/shard_map/ppermute | solution.py:55
  279.7 37.1 %collective-permute-start.41 = (bf16[64,2048]{1,0:T(8,128)(2,1)S(1)}, bf16[64,2048]{1,0:T(8,128)(2,1)S(1)}, u32[]{:S(2)}, u32[]{:S(2)}) collective-permute-start(bf16[64,2048]{1,0:T(8,128)(2,1)S(1)} %get-tuple-element.99), channel_id=1, source_target_pairs={{0,1},{1,0},{2,3},{3,2},{4,5},{5,4},{6,7},{7,6},{8,9},{9,8},{10,11... | collective-permute-start | bytes 786440 | tf_op jit(solution)/shard_map/ppermute | solution.py:55
  306.6 37.2 %collective-permute-start.40 = (bf16[64,2048]{1,0:T(8,128)(2,1)}, bf16[64,2048]{1,0:T(8,128)(2,1)}, u32[]{:S(2)}, u32[]{:S(2)}) collective-permute-start(bf16[64,2048]{1,0:T(8,128)(2,1)} %get-tuple-element.95), channel_id=1, source_target_pairs={{0,1},{1,0},{2,3},{3,2},{4,5},{5,4},{6,7},{7,6},{8,9},{9,8},{10,11... | collective-permute-start | bytes 786440 | tf_op jit(solution)/shard_map/ppermute | solution.py:55
  343.9 20.0 %collective-permute-start.69 = (bf16[64,2048]{1,0:T(8,128)(2,1)}, bf16[64,2048]{1,0:T(8,128)(2,1)S(1)}, u32[]{:S(2)}, u32[]{:S(2)}) collective-permute-start(bf16[64,2048]{1,0:T(8,128)(2,1)} %get-tuple-element.145), channel_id=1, source_target_pairs={{0,1},{1,0},{2,3},{3,2},{4,5},{5,4},{6,7},{7,6},{8,9},{9,8},{10,11... | collective-permute-start | bytes 786440 | tf_op jit(solution)/shard_map/ppermute | solution.py:55
  427.1 33.0 %collective-permute-start.83 = (bf16[64,2048]{1,0:T(8,128)(2,1)}, bf16[64,2048]{1,0:T(8,128)(2,1)S(1)}, u32[]{:S(2)}, u32[]{:S(2)}) collective-permute-start(bf16[64,2048]{1,0:T(8,128)(2,1)} %get-tuple-element.67), channel_id=1, source_target_pairs={{0,1},{1,0},{2,3},{3,2},{4,5},{5,4},{6,7},{7,6},{8,9},{9,8},{10,11... | collective-permute-start | bytes 786440 | tf_op jit(solution)/shard_map/ppermute | solution.py:55
  440.2 21.4 %collective-permute-start.90 = (bf16[64,2048]{1,0:T(8,128)(2,1)}, bf16[64,2048]{1,0:T(8,128)(2,1)}, u32[]{:S(2)}, u32[]{:S(2)}) collective-permute-start(bf16[64,2048]{1,0:T(8,128)(2,1)} %get-tuple-element.68), channel_id=1, source_target_pairs={{0,1},{1,0},{2,3},{3,2},{4,5},{5,4},{6,7},{7,6},{8,9},{9,8},{10,11... | collective-permute-start | bytes 786440 | tf_op jit(solution)/shard_map/ppermute | solution.py:55
  440.4 34.3 %collective-permute-start.101 = (bf16[512,1024]{1,0:T(8,128)(2,1)}, bf16[512,1024]{1,0:T(8,128)(2,1)}, u32[]{:S(2)}, u32[]{:S(2)}) collective-permute-start(bf16[512,1024]{1,0:T(8,128)(2,1)} %constant_dynamic-slice_fusion.2), channel_id=1, source_target_pairs={{0,8},{8,0},{16,24},{24,16},{1,9},{9,1},{17,25},{25,17},{2,10},{10... | collective-permute-start | bytes 3145736 | tf_op jit(solution)/shard_map/ppermute | solution.py:136
  460.1 24.7 %collective-permute-start.103 = (bf16[512,1024]{1,0:T(8,128)(2,1)}, bf16[512,1024]{1,0:T(8,128)(2,1)S(1)}, u32[]{:S(2)}, u32[]{:S(2)}) collective-permute-start(bf16[512,1024]{1,0:T(8,128)(2,1)} %fusion.17), channel_id=1, source_target_pairs={{0,16},{8,24},{16,0},{24,8},{1,17},{9,25},{17,1},{25,9},{2,18},{10... | collective-permute-start | bytes 3145736 | tf_op jit(solution)/shard_map/ppermute | solution.py:136
  461.6 24.8 %collective-permute-start.82 = (bf16[64,2048]{1,0:T(8,128)(2,1)S(1)}, bf16[64,2048]{1,0:T(8,128)(2,1)S(1)}, u32[]{:S(2)}, u32[]{:S(2)}) collective-permute-start(bf16[64,2048]{1,0:T(8,128)(2,1)S(1)} %get-tuple-element.63), channel_id=1, source_target_pairs={{0,1},{1,0},{2,3},{3,2},{4,5},{5,4},{6,7},{7,6},{8,9},{9,8},{10,11... | collective-permute-start | bytes 786440 | tf_op jit(solution)/shard_map/ppermute | solution.py:55
  538.3 21.4 %collective-permute-start.110 = (bf16[256,1024]{1,0:T(8,128)(2,1)S(1)}, bf16[256,1024]{1,0:T(8,128)(2,1)S(1)}, u32[]{:S(2)}, u32[]{:S(2)}) collective-permute-start(bf16[256,1024]{1,0:T(8,128)(2,1)S(1)} %collective-permute-done.108.refs_1_), channel_id=1, source_target_pairs={{0,8},{8,0},{16,24},{24,16},{1,9},{9,1},{17,25},{25,17},{2,10},{10... | collective-permute-start | bytes 1572872 | tf_op jit(solution)/shard_map/ppermute | solution.py:136
  539.3 21.4 %collective-permute-start.113 = (bf16[256,1024]{1,0:T(8,128)(2,1)S(1)}, bf16[256,1024]{1,0:T(8,128)(2,1)}, u32[]{:S(2)}, u32[]{:S(2)}) collective-permute-start(bf16[256,1024]{1,0:T(8,128)(2,1)S(1)} %collective-permute-done.111.refs_5_), channel_id=1, source_target_pairs={{0,16},{8,24},{16,0},{24,8},{1,17},{9,25},{17,1},{25,9},{2,18},{10... | collective-permute-start | bytes 1572872 | tf_op jit(solution)/shard_map/ppermute | solution.py:136
  (165 other events, 2323.4 us)
Sparse Core Ops, SparseCore 0:
  13.7 55.8 all-gather.2
  71.8 49.5 all-gather.4
  273.8 175.6 all-reduce.2
